TPU v7x, 32 devices: a whole 2x2x4 slice. The times are simulated.
32 devices in a mesh: groups: 2 (over x), dp: 16 (over z, y, core).
Axes of the slice: x: 2, y: 2, z: 4, core: 2. Of those that a mesh axis runs over, the one named last changes fastest.
Arguments:
- clips: bfloat16 [128, 4, 49, 1024], P(('groups', 'dp')), parts along dimension 0, may hold values from -6 to 6
- sign_seeds: int32 [128], P(('groups', 'dp')), parts along dimension 0, may hold values from 0 to 999999
- time_weight: bfloat16 [3, 1024, 1024], replicated, may hold values from -0.109375 to 0.109375
- proj_weight: bfloat16 [1024, 512], replicated, may hold values from -0.1875 to 0.1875
- captions: bfloat16 [640, 512], P(('groups', 'dp')), parts along dimension 0, may hold values from -6 to 6
- caption_rows: int32 [128, 5], P(('groups', 'dp')), parts along dimension 0, may hold values from 0 to 319, as said below
Outputs:
- new_delta: bfloat16 [128, 4, 49, 1024], P(('groups', 'dp')), parts along dimension 0
- clip_loss: float32 [128], P(('groups', 'dp')), parts along dimension 0
There are 2 independent parts, one for each index of `groups`. A program takes and returns all parts, laid end to end along the dimension named above; an argument that names none is the same for every part. Nothing has to cross between parts.
Inputs may be any that keep to these rules, and one draw needn't show every extreme that they name: `caption_rows`: the captions of the clips of one dp device are the 20 caption rows of that device; every caption row belongs to exactly one clip.
All inputs are finite; a program needn't handle non-finite values.
Results may differ from a plain program's by a relative error of at most 0.008.
Values may be sent and summed in bfloat16 or wider, within the bound.
No kernel may reach another device: no remote copies, remote signals or barrier semaphores. Data moves between devices by JAX's collectives and lax.ppermute only.
A program may use at most 64 MiB of HBM per device.

v0:
```python
import jax
import jax.numpy as jnp
from jax import lax
from jax.sharding import PartitionSpec as P

INV_TEMP = 1.0 / 0.07


def sign_field(seeds, frames, pix, chans):
    first = lax.broadcasted_iota(jnp.int32, (frames, pix, chans), 0)
    second = lax.broadcasted_iota(jnp.int32, (frames, pix, chans), 1)
    third = lax.broadcasted_iota(jnp.int32, (frames, pix, chans), 2)
    position = (first * pix + second) * chans + third
    mixed = seeds[:, None, None, None] * jnp.int32(-1640531535) + position[None] * jnp.int32(
        374761393
    )
    mixed = mixed ^ mixed >> 13
    mixed = mixed * jnp.int32(668265263)
    mixed = mixed ^ mixed >> 16
    chosen = mixed >> 7 & 1
    return 0.1 * (2 * chosen - 1).astype(jnp.float32)


def temporal(inputs, time_weight):
    frames = inputs.shape[1]
    chans = inputs.shape[3]
    padded = jnp.pad(inputs, ((0, 0), (1, 1), (0, 0), (0, 0)))
    result = jnp.zeros(inputs.shape, jnp.float32)
    for k in range(3):
        window = padded[:, k : k + frames].reshape(-1, chans)
        result = result + jnp.dot(
            window, time_weight[k], preferred_element_type=jnp.float32
        ).reshape(inputs.shape)
    return result


def temporal_back(grad_pre, time_weight):
    frames = grad_pre.shape[1]
    chans = grad_pre.shape[3]
    padded = jnp.pad(grad_pre, ((0, 0), (1, 1), (0, 0), (0, 0)))
    result = jnp.zeros(grad_pre.shape, jnp.float32)
    for k in range(3):
        window = padded[:, 2 - k : 2 - k + frames].reshape(-1, chans)
        result = result + jnp.dot(
            window, time_weight[k].T, preferred_element_type=jnp.float32
        ).reshape(grad_pre.shape)
    return result


def gelu_tanh(value):
    return jax.nn.gelu(value, approximate=True)


def shards(clips, sign_seeds, time_weight, proj_weight, captions, caption_rows):
    clip_dev, frames, pix, chans = clips.shape
    caps_dev = captions.shape[0]
    delta0 = sign_field(sign_seeds, frames, pix, chans)
    inputs = (clips.astype(jnp.float32) + delta0).astype(jnp.bfloat16)
    pre = temporal(inputs, time_weight)
    active, act_back = jax.vjp(gelu_tanh, pre)
    pooled = jnp.mean(active, axis=(1, 2)).astype(jnp.bfloat16)
    video = jnp.dot(pooled, proj_weight, preferred_element_type=jnp.float32)
    vnorm = jnp.sqrt(jnp.sum(video * video, axis=1, keepdims=True) + 1e-06)
    vunit = video / vnorm
    video_hat = vunit.astype(jnp.bfloat16)
    cap32 = captions.astype(jnp.float32)
    caption_hat = (cap32 / jnp.sqrt(jnp.sum(cap32 * cap32, axis=1, keepdims=True) + 1e-06)).astype(
        jnp.bfloat16
    )
    local_rows = caption_rows - lax.axis_index("dp") * caps_dev
    mine = jnp.arange(caps_dev, dtype=jnp.int32)
    own = jnp.sum((local_rows[:, :, None] == mine[None, None, :]).astype(jnp.float32), axis=1)
    block_scores = (
        jnp.dot(
            caption_hat,
            lax.all_gather(video_hat, "dp", axis=0, tiled=True).T,
            preferred_element_type=jnp.float32,
        )
        * INV_TEMP
    )
    colsum = jnp.sum(jnp.exp(block_scores), axis=1)
    scaled = (caption_hat.astype(jnp.float32) / colsum[:, None]).astype(jnp.bfloat16)
    unit_piece = lax.all_gather(caption_hat, "dp", axis=0, tiled=True)
    scaled_piece = lax.all_gather(scaled, "dp", axis=0, tiled=True)
    block_scores = jnp.dot(video_hat, unit_piece.T, preferred_element_type=jnp.float32) * INV_TEMP
    block_expo = jnp.exp(block_scores)
    block_weights = block_expo.astype(jnp.bfloat16)
    total = jnp.sum(block_expo, axis=1)
    a_sum = jnp.dot(block_weights, unit_piece, preferred_element_type=jnp.float32)
    b_sum = jnp.dot(block_weights, scaled_piece, preferred_element_type=jnp.float32)
    local_scores = jnp.dot(video_hat, caption_hat.T, preferred_element_type=jnp.float32) * INV_TEMP
    local_expo = jnp.exp(local_scores)
    positive = jnp.sum(own * local_expo, axis=1)
    text_part = jnp.sum(own * (jnp.log(colsum)[None, :] - local_scores), axis=1)
    clip_loss = jnp.log(total) - jnp.log(positive) + 0.2 * text_part
    pos_sum = jnp.dot(
        (own * local_expo).astype(jnp.bfloat16), caption_hat, preferred_element_type=jnp.float32
    )
    own_sum = jnp.dot(own.astype(jnp.bfloat16), caption_hat, preferred_element_type=jnp.float32)
    grad = INV_TEMP * (
        a_sum / total[:, None] - pos_sum / positive[:, None] + 0.2 * (b_sum - own_sum)
    )
    grad_video = ((grad - vunit * jnp.sum(vunit * grad, axis=1, keepdims=True)) / vnorm).astype(
        jnp.bfloat16
    )
    grad_pooled = jnp.dot(grad_video, proj_weight.T, preferred_element_type=jnp.float32)
    spread = jnp.broadcast_to(grad_pooled[:, None, None, :] / (frames * pix), pre.shape)
    grad_pre = act_back(spread)[0].astype(jnp.bfloat16)
    grad_in = temporal_back(grad_pre, time_weight)
    rms = jnp.sqrt(jnp.mean(grad_in * grad_in, axis=(1, 2, 3), keepdims=True) + 1e-06)
    new_delta = (delta0 + grad_in / rms).astype(jnp.bfloat16)
    return (new_delta, clip_loss)


def solution(mesh):
    in_specs = (
        P(("groups", "dp"), None, None, None),
        P(("groups", "dp")),
        P(),
        P(),
        P(("groups", "dp"), None),
        P(("groups", "dp"), None),
    )
    out_specs = (P(("groups", "dp"), None, None, None), P(("groups", "dp")))
    return jax.shard_map(shards, mesh=mesh, in_specs=in_specs, out_specs=out_specs, check_vma=False)
```

profile of v0, /device:TPU:0, one launch (start us, length us, event | category | flops | bytes accessed | tf_op | source)
XLA Modules:
  0.0 102.4 jit_solution(11251730279128082261)
XLA Ops:
  0.6 0.7 broadcast_multiply_fusion.2
  1.4 0.9 fusion.45
  2.3 0.7 broadcast_subtract_fusion
  3.0 0.1 copy.15
  3.1 0.1 convert_reduce_fusion
  3.1 0.8 fusion.46
  4.0 0.8 fusion.80
  4.8 24.1 %all-gather = bf16[16,20,512]{2,1,0:T(8,128)(2,1)S(1)} all-gather(bf16[1,20,512]{2,1,0:T(8,128)(2,1)S(1)} %fusion.80), channel_id=1, replica_groups=mesh['groups'=2,'dp'=16] {'dp'}, dimensions={0}, use_global_device_ids=true | all-gather | bytes 348160 | tf_op jit(solution)/shard_map/all_gather | solution.py:83
  28.9 0.1 reshape.72
  29.0 0.2 add_multiply_fusion.1
  29.2 5.5 %fusion.18 = f32[4,4,49,1024]{3,2,1,0:T(8,128)S(1)} fusion(bf16[3,1024,1024]{2,1,0:T(8,128)(2,1)} %param.8, bf16[4,4,49,1024]{3,1,2,0:T(4,128)(2,1)} %param.6, s32[4,49,1024]{2,1,0:T(8,128)S(1)} %add_multiply_fusion.1, s32[4]{0:T(128)S(1)} %broadcast_multiply_fusion.2), kind=kOutput, calls=%fused_computation.28 | convolution fusion | flops 1245167616 | bytes 7716880 | tf_op jit(solution)/shard_map/dot_general | solution.py:31
  34.8 3.0 %fusion.22 = f32[4,4,49,1024]{3,2,1,0:T(8,128)S(1)} fusion(bf16[3,1024,1024]{2,1,0:T(8,128)(2,1)S(1)} %bitcast.54, bf16[4,4,49,1024]{3,1,2,0:T(4,128)(2,1)S(1)} %copy-done.2, s32[4,49,1024]{2,1,0:T(8,128)S(1)} %add_multiply_fusion.1, s32[4]{0:T(128)S(1)} %broadcast_multiply_fusion.2), kind=kOutput, calls=%fused_computation.32 | convolution fusion | flops 1245167616 | bytes 7832064 | tf_op jit(solution)/shard_map/dot_general | solution.py:31
  37.8 6.3 %fusion.15 = (f32[4,1024]{1,0:T(4,128)S(1)}, f32[4,4,49,1024]{3,2,1,0:T(8,128)}) fusion(f32[4,4,49,1024]{3,2,1,0:T(8,128)S(1)} %fusion.22, f32[4,4,49,1024]{3,2,1,0:T(8,128)S(1)} %fusion.18, bf16[3,1024,1024]{2,1,0:T(8,128)(2,1)S(1)} %bitcast.54, bf16[4,4,49,1024]{3,1,2,0:T(4,128)(2,1)S(1)} %copy-done.2, s32[4,49,1024]{2,1,0:T(8,128)S(1)} %add_multiply_fusion.1, ...), kind=kOutput, calls=%fused_computation.23 | convolution fusion | flops 1665036288 | bytes 15188480 | tf_op jit(solution)/shard_map/dot_general | solution.py:31
  44.2 0.4 multiply_reduce_fusion.2
  44.5 0.3 fusion.67
  44.9 0.2 convolution_divide_fusion.1
  45.0 0.1 convert_bitcast_fusion
  45.1 17.6 %all-gather.1 = bf16[16,4,512]{2,1,0:T(4,128)(2,1)S(1)} all-gather(bf16[1,4,512]{2,1,0:T(4,128)(2,1)S(1)} %convert_bitcast_fusion), channel_id=1, replica_groups=mesh['groups'=2,'dp'=16] {'dp'}, dimensions={0}, use_global_device_ids=true | all-gather | bytes 69632 | tf_op jit(solution)/shard_map/all_gather | solution.py:76
  62.7 0.2 fusion.43
  63.0 0.3 multiply_reduce_fusion.3
  63.3 0.5 multiply_add_fusion
  63.8 0.1 fusion.42
  63.9 0.1 fusion.47
  64.0 20.1 %all-gather.2 = bf16[16,20,512]{2,1,0:T(8,128)(2,1)S(1)} all-gather(bf16[1,20,512]{2,1,0:T(8,128)(2,1)S(1)} %fusion.47), channel_id=1, replica_groups=mesh['groups'=2,'dp'=16] {'dp'}, dimensions={0}, use_global_device_ids=true | all-gather | bytes 348160 | tf_op jit(solution)/shard_map/all_gather | solution.py:84
  84.2 0.1 fusion.55
  84.3 0.2 multiply_reduce_fusion.1
  84.6 0.4 broadcast_multiply_fusion
  85.0 5.8 %fusion.16 = f32[4,4,49,1024]{3,2,1,0:T(8,128)S(1)} fusion(bf16[3,1024,1024]{2,1,0:T(8,128)(2,1)} %param.8, f32[4,4,49,1024]{3,2,1,0:T(8,128)} %get-tuple-element.15, f32[4,1024]{1,0:T(4,128)S(1)} %get-tuple-element.13, f32[4,1024]{1,0:T(4,128)S(1)} %get-tuple-element.12), kind=kOutput, calls=%fused_computation.26 | convolution fusion | flops 1248378880 | bytes 9011200 | tf_op jit(solution)/shard_map/dot_general | solution.py:44
  90.8 3.2 %fusion.20 = f32[4,4,49,1024]{3,2,1,0:T(8,128)S(1)} fusion(bf16[3,1024,1024]{2,1,0:T(8,128)(2,1)S(1)} %bitcast.56, f32[4,4,49,1024]{3,2,1,0:T(8,128)S(1)} %copy-done.3, f32[4,1024]{1,0:T(4,128)S(1)} %get-tuple-element.13, f32[4,1024]{1,0:T(4,128)S(1)} %get-tuple-element.12), kind=kOutput, calls=%fused_computation.30 | convolution fusion | flops 1248378880 | bytes 9011200 | tf_op jit(solution)/shard_map/dot_general | solution.py:44
  94.1 4.1 %multiply_reduce_fusion = (f32[4]{0:T(128)S(1)}, f32[4,4,49,1024]{3,2,1,0:T(8,128)S(1)}) fusion(f32[4,4,49,1024]{3,2,1,0:T(8,128)S(1)} %fusion.20, f32[4,4,49,1024]{3,2,1,0:T(8,128)S(1)} %fusion.16, bf16[3,1024,1024]{2,1,0:T(8,128)(2,1)S(1)} %bitcast.56, f32[4,4,49,1024]{3,2,1,0:T(8,128)S(1)} %copy-done.3, f32[4,1024]{1,0:T(4,128)S(1)} %get-tuple-element.13, ...), kind=kOutput, calls=%fused_computation.19 | convolution fusion | flops 1662631936 | bytes 16351248 | tf_op jit(solution)/shard_map/dot_general | solution.py:44
  98.2 1.8 %add_convert_fusion = bf16[4,4,49,1024]{3,2,1,0:T(8,128)(2,1)S(1)} fusion(f32[4,4,49,1024]{3,2,1,0:T(8,128)S(1)} %get-tuple-element.24, f32[4]{0:T(128)S(1)} %add_sqrt_fusion, s32[4,49,1024]{2,1,0:T(8,128)S(1)} %add_multiply_fusion.1, s32[4]{0:T(128)S(1)} %broadcast_multiply_fusion.2), kind=kLoop, calls=%fused_computation.18 | loop fusion | flops 12042240 | bytes 5619744 | tf_op jit(solution)/shard_map/convert_element_type | solution.py:111
  100.0 2.4 %copy.16 = bf16[4,4,49,1024]{3,1,2,0:T(4,128)(2,1)} copy(bf16[4,4,49,1024]{3,2,1,0:T(8,128)(2,1)S(1)} %add_convert_fusion) | data formatting | bytes 3211264
  (25 shorter events, 0.2 us)
Async XLA Ops:
  0.6 43.5 %copy-start = (bf16[1024,512]{1,0:T(8,128)(2,1)S(1)}, bf16[1024,512]{1,0:T(8,128)(2,1)}, u32[]{:S(2)}) copy-start(bf16[1024,512]{1,0:T(8,128)(2,1)} %param.9) | copy-start | bytes 3145732
  29.0 5.8 %slice-start = ((s8[6291456]{0:T(1024)(128)(4,1)}), s8[4194304]{0:T(1024)(128)(4,1)S(1)}, s32[]{:S(2)}) async-start(s8[6291456]{0:T(1024)(128)(4,1)} %bitcast.53), calls=%async_computation | async-start | bytes 8388608
  29.2 5.6 %slice-start.1 = ((s8[6291456]{0:T(1024)(128)(4,1)}), s8[2097152]{0:T(1024)(128)(4,1)S(1)}, s32[]{:S(2)}) async-start(s8[6291456]{0:T(1024)(128)(4,1)} %bitcast.53), calls=%async_computation.1 | async-start | bytes 4194304
  29.2 5.6 %copy-start.2 = (bf16[4,4,49,1024]{3,1,2,0:T(4,128)(2,1)S(1)}, bf16[4,4,49,1024]{3,1,2,0:T(4,128)(2,1)}, u32[]{:S(2)}) copy-start(bf16[4,4,49,1024]{3,1,2,0:T(4,128)(2,1)} %param.6) | copy-start | bytes 4816900
  37.8 26.1 %copy-start.1 = (bf16[20,512]{1,0:T(8,128)(2,1)S(1)}, bf16[20,512]{1,0:T(8,128)(2,1)}, u32[]{:S(2)}) copy-start(bf16[20,512]{1,0:T(8,128)(2,1)} %param.10) | copy-start | bytes 61444
  84.6 6.2 %slice-start.2 = ((s8[6291456]{0:T(1024)(128)(4,1)}), s8[4194304]{0:T(1024)(128)(4,1)S(1)}, s32[]{:S(2)}) async-start(s8[6291456]{0:T(1024)(128)(4,1)} %bitcast.55), calls=%async_computation.2 | async-start | bytes 8388608
  85.0 5.8 %slice-start.3 = ((s8[6291456]{0:T(1024)(128)(4,1)}), s8[2097152]{0:T(1024)(128)(4,1)S(1)}, s32[]{:S(2)}) async-start(s8[6291456]{0:T(1024)(128)(4,1)} %bitcast.55), calls=%async_computation.3 | async-start | bytes 4194304
  85.0 5.8 %copy-start.3 = (f32[4,4,49,1024]{3,2,1,0:T(8,128)S(1)}, f32[4,4,49,1024]{3,2,1,0:T(8,128)}, u32[]{:S(2)}) copy-start(f32[4,4,49,1024]{3,2,1,0:T(8,128)} %get-tuple-element.15) | copy-start | bytes 9633796
where the time goes:
time: 103 us; the launch traced here: 102 us
  blocking collectives  61.8 us (60%)
  matrix products  30.3 us (29%)
  other arithmetic  6.73 us (7%)
  local copies, waits for them, and re-layouts  2.72 us (3%)
    all_gather x1, blocking collectives, shards(): unit_piece = lax.all_gather(caption_hat, 'dp', axis=0, tiled=True)  24.1 us
    all_gather x1, blocking collectives, shards(): scaled_piece = lax.all_gather(scaled, 'dp', axis=0, tiled=True)  20.1 us
    all_gather x1, blocking collectives, shards(): lax.all_gather(video_hat, 'dp', axis=0, tiled=True)  17.6 us
    dot_general x3, matrix products, temporal(): jnp.dot(window, time_weight[k], preferred_element_type=jnp.float32)  14.9 us
    dot_general x3, matrix products, temporal_back(): jnp.dot(window, time_weight[k].T, preferred_element_type=jnp.float32)  13.1 us
    unnamed x20, local copies, waits for them, and re-layouts  2.62 us

commit v1 on v0

v1 whole, which is shorter than its diff:
```python
import functools

import jax
import jax.numpy as jnp
from jax import lax
from jax.experimental import pallas as pl
from jax.experimental.pallas import tpu as pltpu
from jax.sharding import PartitionSpec as P

INV_TEMP = 1.0 / 0.07
GELU_A = 0.7978845608028654
GELU_B = 0.044715
VMEM_LIMIT = 48 << 20


def sign_rows(seed, first_row, rows, frames, pix, chans):
    row = lax.broadcasted_iota(jnp.int32, (rows, 1), 0) + first_row
    pixel = row // frames
    frame = row - pixel * frames
    start = (frame * pix + pixel) * chans * jnp.int32(374761393) + seed * jnp.int32(-1640531535)
    column = lax.broadcasted_iota(jnp.int32, (1, chans), 1) * jnp.int32(374761393)
    mixed = start + column
    mixed = mixed ^ (mixed >> 13)
    mixed = mixed * jnp.int32(668265263)
    mixed = mixed ^ (mixed >> 16)
    return jnp.where((mixed & 128) != 0, jnp.float32(0.1), jnp.float32(-0.1))


def taps(value, frames):
    rows = value.shape[0]
    frame = lax.broadcasted_iota(jnp.int32, (rows, 1), 0) % frames
    before = jnp.where(frame > 0, pltpu.roll(value, 1, 0), 0.0)
    after = jnp.where(frame < frames - 1, pltpu.roll(value, rows - 1, 0), 0.0)
    return before, after


def forward_kernel(dims, seeds, clips, weight, proj, captions, pack, unit, slope, lhs, pre, joined):
    clip_dev, frames, pix, chans, pad = dims
    real = frames * pix
    for i in range(clip_dev):
        base = i * pad
        x = clips[i].astype(jnp.float32).reshape(real, chans)
        x = x + sign_rows(seeds[i], 0, real, frames, pix, chans)
        x = jnp.concatenate([x, jnp.zeros((pad - real, chans), jnp.float32)], 0)
        x = x.astype(jnp.bfloat16).astype(jnp.float32)
        before, after = taps(x, frames)
        lhs[base : base + pad, 0:chans] = before.astype(jnp.bfloat16)
        lhs[base : base + pad, chans : 2 * chans] = x.astype(jnp.bfloat16)
        lhs[base : base + pad, 2 * chans : 3 * chans] = after.astype(jnp.bfloat16)
    pre[...] = jnp.dot(lhs[...], weight[...], preferred_element_type=jnp.float32)
    sums = []
    for i in range(clip_dev):
        v = pre[i * pad : (i + 1) * pad, :]
        square = v * v
        t = jnp.tanh(GELU_A * v * (1.0 + GELU_B * square))
        half = 0.5 + 0.5 * t
        sums.append(jnp.sum(v * half, axis=0, keepdims=True))
        inner = GELU_A * (1.0 + 3.0 * GELU_B * square)
        slope[i * pad : (i + 1) * pad, :] = (half + 0.5 * v * (1.0 - t * t) * inner).astype(jnp.bfloat16)
    pooled = (jnp.concatenate(sums + sums, 0) * (1.0 / real)).astype(jnp.bfloat16)
    video = jnp.dot(pooled, proj[...], preferred_element_type=jnp.float32)
    vnorm = jnp.sqrt(jnp.sum(video * video, axis=1, keepdims=True) + 1e-06)
    vunit = video / vnorm
    unit[0:8, :] = vunit
    unit[8:16, :] = jnp.broadcast_to(vnorm, vunit.shape)
    cap = captions[...].astype(jnp.float32)
    cap = cap / jnp.sqrt(jnp.sum(cap * cap, axis=1, keepdims=True) + 1e-06)
    caps_dev = cap.shape[0]
    joined[0:caps_dev, :] = cap
    joined[caps_dev : caps_dev + clip_dev, :] = vunit[0:clip_dev]
    pack[...] = joined[...].astype(jnp.bfloat16)


def backward_kernel(dims, seeds, rows, every, unit, slope, weight, proj, out, loss, lhs, colsum):
    clip_dev, frames, pix, chans, pad, caps_dev, blocks = dims
    real = frames * pix
    group = caps_dev + clip_dev
    wide = every.shape[0]
    step = 16 * group
    colsum[...] = jnp.zeros_like(colsum)

    def part(b, carry):
        block = every[pl.ds(pl.multiple_of(b * step, step), step), :]
        s = lax.dot_general(block, every[...], (((1,), (1,)), ((), ())), preferred_element_type=jnp.float32)
        row = lax.broadcasted_iota(jnp.int32, (step, 1), 0) % group
        colsum[...] += jnp.sum(jnp.where(row >= caps_dev, jnp.exp(s * INV_TEMP), 0.0), axis=0, keepdims=True)
        return carry

    lax.fori_loop(0, wide // step, part, 0)
    mine = every[group - 8 : group, :]
    scores = lax.dot_general(mine, every[...], (((1,), (1,)), ((), ())), preferred_element_type=jnp.float32) * INV_TEMP
    column = lax.broadcasted_iota(jnp.int32, (1, wide), 1)
    line = lax.broadcasted_iota(jnp.int32, (8, 1), 0)
    expo = jnp.where(column % group < caps_dev, jnp.exp(scores), 0.0)
    own = jnp.zeros((8, wide), jnp.float32)
    for i in range(clip_dev):
        for c in range(rows.shape[1]):
            local = lax.rem(rows[i, c], caps_dev)
            own = own + jnp.where((line == 8 - clip_dev + i) & (column == local), 1.0, 0.0)
    sums = colsum[...]
    sums = jnp.where(column % group < caps_dev, sums, 1.0)
    total = jnp.sum(expo, axis=1, keepdims=True)
    owned = own * expo
    positive = jnp.sum(owned, axis=1, keepdims=True)
    text = jnp.sum(own * (jnp.log(sums) - scores), axis=1, keepdims=True)
    safe = jnp.where(line >= 8 - clip_dev, positive, 1.0)
    value = jnp.log(total) - jnp.log(safe) + 0.2 * text
    place = lax.broadcasted_iota(jnp.int32, (8, 128), 1) + (8 - clip_dev)
    picked = jnp.sum(jnp.where(place == line, value, 0.0), axis=0, keepdims=True)
    loss[...] = picked[:, 0:clip_dev]
    coef = expo / total - owned / safe + 0.2 * (expo / sums - own)
    grad = INV_TEMP * jnp.dot(coef.astype(jnp.bfloat16), every[...], preferred_element_type=jnp.float32)
    vunit = unit[0:8, :]
    vnorm = unit[8:16, :]
    grad_video = ((grad - vunit * jnp.sum(vunit * grad, axis=1, keepdims=True)) / vnorm).astype(jnp.bfloat16)
    grad_pooled = lax.dot_general(
        grad_video, proj[...], (((1,), (1,)), ((), ())), preferred_element_type=jnp.float32
    ) * (1.0 / real)
    for i in range(clip_dev):
        base = i * pad
        g = grad_pooled[8 - clip_dev + i : 8 - clip_dev + i + 1, :]
        gp = slope[base : base + pad, :].astype(jnp.float32) * g
        keep = lax.broadcasted_iota(jnp.int32, (pad, 1), 0) < real
        gp = jnp.where(keep, gp, 0.0)
        before, after = taps(gp, frames)
        lhs[base : base + pad, 0:chans] = after.astype(jnp.bfloat16)
        lhs[base : base + pad, chans : 2 * chans] = gp.astype(jnp.bfloat16)
        lhs[base : base + pad, 2 * chans : 3 * chans] = before.astype(jnp.bfloat16)
    for i in range(clip_dev):
        base = i * pad
        acc = jnp.zeros((pad, chans), jnp.float32)
        for k in range(3):
            acc = acc + lax.dot_general(
                lhs[base : base + pad, k * chans : (k + 1) * chans],
                weight[k],
                (((1,), (1,)), ((), ())),
                preferred_element_type=jnp.float32,
            )
        scale = lax.rsqrt(jnp.sum(acc * acc) / (real * chans) + 1e-06)
        delta = sign_rows(seeds[i], 0, pad, frames, pix, chans) + acc * scale
        out[i] = delta[0:real].reshape(pix, frames, chans).astype(jnp.bfloat16)


def exchange(pack, blocks):
    held = pack
    step = blocks // 2
    while step:
        pairs = [(i, i ^ step) for i in range(blocks)]
        held = jnp.concatenate([held, lax.ppermute(held, "dp", pairs)], 0)
        step //= 2
    return held


def shards(blocks, clips, sign_seeds, time_weight, proj_weight, captions, caption_rows):
    clip_dev, frames, pix, chans = clips.shape
    caps_dev, embed = captions.shape
    pad = -(-frames * pix // 16) * 16
    vmem = pl.BlockSpec(memory_space=pltpu.VMEM)
    smem = pl.BlockSpec(memory_space=pltpu.SMEM)
    params = pltpu.CompilerParams(vmem_limit_bytes=VMEM_LIMIT)
    group = caps_dev + clip_dev
    pack, unit, slope = pl.pallas_call(
        functools.partial(forward_kernel, (clip_dev, frames, pix, chans, pad)),
        out_shape=(
            jax.ShapeDtypeStruct((group, embed), jnp.bfloat16),
            jax.ShapeDtypeStruct((16, embed), jnp.float32),
            jax.ShapeDtypeStruct((clip_dev * pad, chans), jnp.bfloat16),
        ),
        in_specs=[smem, vmem, vmem, vmem, vmem],
        out_specs=(vmem, vmem, vmem),
        scratch_shapes=[
            pltpu.VMEM((clip_dev * pad, 3 * chans), jnp.bfloat16),
            pltpu.VMEM((clip_dev * pad, chans), jnp.float32),
            pltpu.VMEM((group, embed), jnp.float32),
        ],
        compiler_params=params,
        name="forward",
    )(
        sign_seeds,
        clips.transpose(0, 2, 1, 3),
        time_weight.reshape(3 * chans, chans),
        proj_weight,
        captions,
    )
    every = exchange(pack, blocks)
    delta, loss = pl.pallas_call(
        functools.partial(backward_kernel, (clip_dev, frames, pix, chans, pad, caps_dev, blocks)),
        out_shape=(
            jax.ShapeDtypeStruct((clip_dev, pix, frames, chans), jnp.bfloat16),
            jax.ShapeDtypeStruct((1, clip_dev), jnp.float32),
        ),
        in_specs=[smem, smem, vmem, vmem, vmem, vmem, vmem],
        out_specs=(vmem, vmem),
        scratch_shapes=[
            pltpu.VMEM((clip_dev * pad, 3 * chans), jnp.bfloat16),
            pltpu.VMEM((1, blocks * group), jnp.float32),
        ],
        compiler_params=params,
        name="backward",
    )(sign_seeds, caption_rows, every, unit, slope, time_weight, proj_weight)
    return delta.transpose(0, 2, 1, 3), loss.reshape(clip_dev)


def solution(mesh):
    in_specs = (
        P(("groups", "dp"), None, None, None),
        P(("groups", "dp")),
        P(),
        P(),
        P(("groups", "dp"), None),
        P(("groups", "dp"), None),
    )
    out_specs = (P(("groups", "dp"), None, None, None), P(("groups", "dp")))
    return jax.shard_map(
        functools.partial(shards, mesh.shape["dp"]),
        mesh=mesh,
        in_specs=in_specs,
        out_specs=out_specs,
        check_vma=False,
    )
```

time: 103 us -> 47.2 us (0.46)
  blocking collectives: 61.8 us -> 0 us
  matrix products: 30.3 us -> 0 us
  Pallas kernels: 0 us -> 25.9 us
  starting transfers between devices: 0 us -> 8.12 us
  waiting for transfers between devices: 0 us -> 8.03 us
  other arithmetic: 6.73 us -> 0.03 us
  local copies, waits for them, and re-layouts: 2.72 us -> 4.07 us
    all_gather x3 -> x0, blocking collectives: 61.8 us -> none  [the longest x1 24.1 us: shards(): unit_piece = lax.all_gather(caption_hat, 'dp', axis=0, tiled=True)]
    dot_general x15 -> x0, matrix products: 30.3 us -> none  [the longest x3 14.9 us: temporal(): jnp.dot(window, time_weight[k], preferred_element_type=jnp.float32)]
    pallas_call x0 -> x2, Pallas kernels: none -> 25.9 us  [the longest x1 14.9 us: shards(): pl.pallas_call(functools.partial(backward_kernel, (clip_dev, frames, pix,...]
    ppermute x0 -> x4, starting transfers between devices: none -> 8.12 us  [exchange(): held = jnp.concatenate([held, lax.ppermute(held, 'dp', pairs)], 0)]
    ppermute x0 -> x4, waiting for transfers between devices: none -> 8.03 us  [exchange(): held = jnp.concatenate([held, lax.ppermute(held, 'dp', pairs)], 0)]
    convert_element_type x2 -> x0, other arithmetic: 2.65 us -> none  [the longest x1 1.83 us: shards(): new_delta = (delta0 + grad_in / rms).astype(jnp.bfloat16)]
    unnamed x20 -> x16, local copies, waits for them, and re-layouts: 2.62 us -> 4.06 us
  transfers between devices with their start and end apart: 0 -> 4, of which waited for: 0 -> 4; matrix products, arithmetic and copies ran while one was open for 0% -> 0% of each run, Pallas kernels for 0% -> 0%
where the time goes in v1:
time: 47.2 us; the launch traced here: 46.8 us
  Pallas kernels  25.9 us (55%)
  starting transfers between devices  8.12 us (17%)
  waiting for transfers between devices  8.03 us (17%)
  local copies, waits for them, and re-layouts  4.07 us (9%)
  between operations  0.71 us (2%)
    pallas_call x1, Pallas kernels, shards(): pl.pallas_call(functools.partial(backward_kernel, (clip_dev, frames, pix,...  14.9 us
    pallas_call x1, Pallas kernels, shards(): pl.pallas_call(functools.partial(forward_kernel, (clip_dev, frames, pix,...  11 us
    ppermute x4, starting transfers between devices, exchange(): held = jnp.concatenate([held, lax.ppermute(held, 'dp', pairs)], 0)  8.12 us
    ppermute x4, waiting for transfers between devices, exchange(): held = jnp.concatenate([held, lax.ppermute(held, 'dp', pairs)], 0)  8.03 us
    unnamed x16, local copies, waits for them, and re-layouts  4.06 us
  transfers between devices with their start and end apart: 4, of which 4 were waited for; matrix products, arithmetic and copies ran while one was open for 0% of the time, Pallas kernels for 0%

profile of v1, /device:TPU:0, one launch (start us, length us, event | category | flops | bytes accessed | tf_op | source)
XLA Modules:
  0.0 46.8 jit_solution(4387109283860213554)
XLA Ops:
  0.6 0.0 copy-start
  0.6 1.2 %copy-done = bf16[1024,512]{1,0:T(8,128)(2,1)S(1)} copy-done((bf16[1024,512]{1,0:T(8,128)(2,1)S(1)}, bf16[1024,512]{1,0:T(8,128)(2,1)}, u32[]{:S(2)}) %copy-start) | copy-done | bytes 1048600
  1.9 0.0 copy-start.2
  1.9 1.4 %copy-done.2 = bf16[4,4,49,1024]{3,1,2,0:T(4,128)(2,1)S(1)} copy-done((bf16[4,4,49,1024]{3,1,2,0:T(4,128)(2,1)S(1)}, bf16[4,4,49,1024]{3,1,2,0:T(4,128)(2,1)}, u32[]{:S(2)}) %copy-start.2) | copy-done | bytes 1605656
  3.3 0.0 copy-start.3
  3.3 0.7 %copy-done.3 = bf16[20,512]{1,0:T(8,128)(2,1)S(1)} copy-done((bf16[20,512]{1,0:T(8,128)(2,1)S(1)}, bf16[20,512]{1,0:T(8,128)(2,1)}, u32[]{:S(2)}) %copy-start.3) | copy-done | bytes 20504
  4.0 0.0 copy-start.5
  4.0 0.7 %copy-done.5 = s32[4]{0:T(128)S(1)} copy-done((s32[4]{0:T(128)S(1)}, s32[4]{0:T(128)}, u32[]{:S(2)}) %copy-start.5) | copy-done | bytes 40
  4.7 0.0 copy-start.4
  4.7 11.0 %forward.1 = (bf16[24,512]{1,0:T(8,128)(2,1)S(1)}, f32[16,512]{1,0:T(8,128)S(1)}, bf16[832,1024]{1,0:T(8,128)(2,1)S(1)}) custom-call(s32[4]{0:T(128)S(1)} %copy-done.5, bf16[4,49,4,1024]{3,2,1,0:T(4,128)(2,1)S(1)} %bitcast.4, bf16[3072,1024]{1,0:T(8,128)(2,1)} %bitcast.5, bf16[1024,512]{1,0:T(8,128)(2,1)S(1)} %copy-done, bf16[20,512]{1,0:T(8,128)(2,1)S(1)} %copy-done.3), custom_call_target="tpu_custom_call" | custom-call | tf_op jit(solution)/shard_map/forward/pallas_call | solution.py:162
  15.7 0.0 copy-start.1
  15.7 4.1 %collective-permute-start = (bf16[24,512]{1,0:T(8,128)(2,1)S(1)}, bf16[24,512]{1,0:T(8,128)(2,1)S(1)}, u32[]{:S(2)}, u32[]{:S(2)}) collective-permute-start(bf16[24,512]{1,0:T(8,128)(2,1)S(1)} %get-tuple-element.7), channel_id=1, source_target_pairs={{0,8},{1,9},{2,10},{3,11},{4,12},{5,13},{6,14},{7,15},{8,0},{9,1},... | collective-permute-start | bytes 73736 | tf_op jit(solution)/shard_map/ppermute | solution.py:149
  19.8 1.8 %collective-permute-done = bf16[24,512]{1,0:T(8,128)(2,1)S(1)} collective-permute-done((bf16[24,512]{1,0:T(8,128)(2,1)S(1)}, bf16[24,512]{1,0:T(8,128)(2,1)S(1)}, u32[]{:S(2)}, u32[]{:S(2)}) %collective-permute-start) | collective-permute-done | bytes 24608 | tf_op jit(solution)/shard_map/ppermute | solution.py:149
  21.6 1.9 %collective-permute-start.1 = (bf16[48,512]{1,0:T(8,128)(2,1)S(1)}, bf16[48,512]{1,0:T(8,128)(2,1)S(1)}, u32[]{:S(2)}, u32[]{:S(2)}) collective-permute-start(bf16[48,512]{1,0:T(8,128)(2,1)S(1)} %pad_maximum_fusion.2), channel_id=1, source_target_pairs={{0,4},{1,5},{2,6},{3,7},{4,0},{5,1},{6,2},{7,3},{8,12},{9,13},{10,... | collective-permute-start | bytes 147464 | tf_op jit(solution)/shard_map/ppermute | solution.py:149
  23.5 2.2 %collective-permute-done.1 = bf16[48,512]{1,0:T(8,128)(2,1)S(1)} collective-permute-done((bf16[48,512]{1,0:T(8,128)(2,1)S(1)}, bf16[48,512]{1,0:T(8,128)(2,1)S(1)}, u32[]{:S(2)}, u32[]{:S(2)}) %collective-permute-start.1) | collective-permute-done | bytes 49184 | tf_op jit(solution)/shard_map/ppermute | solution.py:149
  25.7 2.0 %collective-permute-start.2 = (bf16[96,512]{1,0:T(8,128)(2,1)S(1)}, bf16[96,512]{1,0:T(8,128)(2,1)S(1)}, u32[]{:S(2)}, u32[]{:S(2)}) collective-permute-start(bf16[96,512]{1,0:T(8,128)(2,1)S(1)} %pad_maximum_fusion.1), channel_id=1, source_target_pairs={{0,2},{1,3},{2,0},{3,1},{4,6},{5,7},{6,4},{7,5},{8,10},{9,11},{10,... | collective-permute-start | bytes 294920 | tf_op jit(solution)/shard_map/ppermute | solution.py:149
  27.7 2.6 %collective-permute-done.2 = bf16[96,512]{1,0:T(8,128)(2,1)S(1)} collective-permute-done((bf16[96,512]{1,0:T(8,128)(2,1)S(1)}, bf16[96,512]{1,0:T(8,128)(2,1)S(1)}, u32[]{:S(2)}, u32[]{:S(2)}) %collective-permute-start.2) | collective-permute-done | bytes 98336 | tf_op jit(solution)/shard_map/ppermute | solution.py:149
  30.4 0.1 collective-permute-start.3
  30.5 1.4 %collective-permute-done.3 = bf16[192,512]{1,0:T(8,128)(2,1)S(1)} collective-permute-done((bf16[192,512]{1,0:T(8,128)(2,1)S(1)}, bf16[192,512]{1,0:T(8,128)(2,1)S(1)}, u32[]{:S(2)}, u32[]{:S(2)}) %collective-permute-start.3) | collective-permute-done | bytes 196640 | tf_op jit(solution)/shard_map/ppermute | solution.py:149
  31.9 0.0 copy-done.4
  31.9 0.0 copy-done.1
  31.9 14.9 %backward.1 = (bf16[4,49,4,1024]{3,2,1,0:T(4,128)(2,1)}, f32[1,4]{1,0:T(1,128)}) custom-call(s32[4]{0:T(128)S(1)} %copy-done.5, s32[4,5]{1,0:T(4,128)S(1)} %copy-done.4, bf16[384,512]{1,0:T(8,128)(2,1)S(1)} %constant_dynamic-update-slice_fusion.every, f32[16,512]{1,0:T(8,128)S(1)} %get-tuple-element.8.unit, bf16[832,1024]{1,0:T(8,128)(2,1)S(1)} %get-tuple-element.9.slope, ...), custom_call_target="tpu_custom_call" | custom-call | tf_op jit(solution)/shard_map/backward/pallas_call | solution.py:186
  (8 shorter events, 0.1 us)
Async XLA Ops:
  0.6 1.2 %copy-start = (bf16[1024,512]{1,0:T(8,128)(2,1)S(1)}, bf16[1024,512]{1,0:T(8,128)(2,1)}, u32[]{:S(2)}) copy-start(bf16[1024,512]{1,0:T(8,128)(2,1)} %proj.3) | copy-start | bytes 3145732
  1.9 1.4 %copy-start.2 = (bf16[4,4,49,1024]{3,1,2,0:T(4,128)(2,1)S(1)}, bf16[4,4,49,1024]{3,1,2,0:T(4,128)(2,1)}, u32[]{:S(2)}) copy-start(bf16[4,4,49,1024]{3,1,2,0:T(4,128)(2,1)} %param.6) | copy-start | bytes 4816900
  3.3 0.7 %copy-start.3 = (bf16[20,512]{1,0:T(8,128)(2,1)S(1)}, bf16[20,512]{1,0:T(8,128)(2,1)}, u32[]{:S(2)}) copy-start(bf16[20,512]{1,0:T(8,128)(2,1)} %captions.1) | copy-start | bytes 61444
  4.0 0.7 %copy-start.5 = (s32[4]{0:T(128)S(1)}, s32[4]{0:T(128)}, u32[]{:S(2)}) copy-start(s32[4]{0:T(128)} %seeds.3) | copy-start | bytes 52
  4.7 27.3 %copy-start.4 = (s32[4,5]{1,0:T(4,128)S(1)}, s32[4,5]{1,0:T(4,128)}, u32[]{:S(2)}) copy-start(s32[4,5]{1,0:T(4,128)} %rows.1) | copy-start | bytes 244
  15.7 16.3 %copy-start.1 = (bf16[1024,512]{1,0:T(8,128)(2,1)S(1)}, bf16[1024,512]{1,0:T(8,128)(2,1)}, u32[]{:S(2)}) copy-start(bf16[1024,512]{1,0:T(8,128)(2,1)} %proj.3) | copy-start | bytes 3145732
  15.7 5.9 %collective-permute-start = (bf16[24,512]{1,0:T(8,128)(2,1)S(1)}, bf16[24,512]{1,0:T(8,128)(2,1)S(1)}, u32[]{:S(2)}, u32[]{:S(2)}) collective-permute-start(bf16[24,512]{1,0:T(8,128)(2,1)S(1)} %get-tuple-element.7), channel_id=1, source_target_pairs={{0,8},{1,9},{2,10},{3,11},{4,12},{5,13},{6,14},{7,15},{8,0},{9,1},... | collective-permute-start | bytes 73736 | tf_op jit(solution)/shard_map/ppermute | solution.py:149
  21.6 4.1 %collective-permute-start.1 = (bf16[48,512]{1,0:T(8,128)(2,1)S(1)}, bf16[48,512]{1,0:T(8,128)(2,1)S(1)}, u32[]{:S(2)}, u32[]{:S(2)}) collective-permute-start(bf16[48,512]{1,0:T(8,128)(2,1)S(1)} %pad_maximum_fusion.2), channel_id=1, source_target_pairs={{0,4},{1,5},{2,6},{3,7},{4,0},{5,1},{6,2},{7,3},{8,12},{9,13},{10,... | collective-permute-start | bytes 147464 | tf_op jit(solution)/shard_map/ppermute | solution.py:149
  25.7 4.7 %collective-permute-start.2 = (bf16[96,512]{1,0:T(8,128)(2,1)S(1)}, bf16[96,512]{1,0:T(8,128)(2,1)S(1)}, u32[]{:S(2)}, u32[]{:S(2)}) collective-permute-start(bf16[96,512]{1,0:T(8,128)(2,1)S(1)} %pad_maximum_fusion.1), channel_id=1, source_target_pairs={{0,2},{1,3},{2,0},{3,1},{4,6},{5,7},{6,4},{7,5},{8,10},{9,11},{10,... | collective-permute-start | bytes 294920 | tf_op jit(solution)/shard_map/ppermute | solution.py:149
  30.4 1.5 %collective-permute-start.3 = (bf16[192,512]{1,0:T(8,128)(2,1)S(1)}, bf16[192,512]{1,0:T(8,128)(2,1)S(1)}, u32[]{:S(2)}, u32[]{:S(2)}) collective-permute-start(bf16[192,512]{1,0:T(8,128)(2,1)S(1)} %pad_maximum_fusion), channel_id=1, source_target_pairs={{0,1},{1,0},{2,3},{3,2},{4,5},{5,4},{6,7},{7,6},{8,9},{9,8},{10,11... | collective-permute-start | bytes 589832 | tf_op jit(solution)/shard_map/ppermute | solution.py:149

commit v2 on v1

v2 whole, which is shorter than its diff:
```python
import functools

import jax
import jax.numpy as jnp
from jax import lax
from jax.experimental import pallas as pl
from jax.experimental.pallas import tpu as pltpu
from jax.sharding import PartitionSpec as P

INV_TEMP = 1.0 / 0.07
GELU_A = 0.7978845608028654
GELU_B = 0.044715
VMEM_LIMIT = 28 << 20
SLOPE_LIMIT = 8 << 20


def sign_rows(seed, first_row, rows, frames, pix, chans):
    row = lax.broadcasted_iota(jnp.int32, (rows, 1), 0) + first_row
    pixel = row // frames
    frame = row - pixel * frames
    start = (frame * pix + pixel) * chans * jnp.int32(374761393) + seed * jnp.int32(-1640531535)
    column = lax.broadcasted_iota(jnp.int32, (1, chans), 1) * jnp.int32(374761393)
    mixed = start + column
    mixed = mixed ^ (mixed >> 13)
    mixed = mixed * jnp.int32(668265263)
    mixed = mixed ^ (mixed >> 16)
    return jnp.where((mixed & 128) != 0, jnp.float32(0.1), jnp.float32(-0.1))


def clip_of(shape, dim, slot, clip_dev):
    row = lax.broadcasted_iota(jnp.int32, shape, dim)
    return jnp.where(row % slot < slot - 1, row // slot, clip_dev)


def exact_dot(a, b):
    return jnp.dot(a, b, preferred_element_type=jnp.float32, precision=lax.Precision.HIGHEST)


def forward_kernel(
    dims, seeds_hbm, clips_hbm, weight_hbm, proj_hbm, captions_hbm, pack, unit, pre,
    seeds, clips, weight, proj, captions, natural, lhs, joined, sems,
):
    clip_dev, frames, pix, chans, slot = dims
    real, padded, block = frames * pix, frames * slot, clip_dev * slot
    caps_dev = captions.shape[0]
    copies = [pltpu.make_async_copy(seeds_hbm, seeds, sems.at[0])]
    copies += [pltpu.make_async_copy(clips_hbm.at[i], clips.at[i], sems.at[1 + i]) for i in range(clip_dev)]
    copies += [pltpu.make_async_copy(captions_hbm, captions, sems.at[1 + clip_dev])]
    copies += [pltpu.make_async_copy(weight_hbm.at[k], weight.at[k], sems.at[2 + clip_dev + k]) for k in (1, 0, 2)]
    copies += [pltpu.make_async_copy(proj_hbm, proj, sems.at[5 + clip_dev])]
    for copy in copies:
        copy.start()
    copies[0].wait()
    for i in range(clip_dev):
        copies[1 + i].wait()
        x = clips[i].astype(jnp.float32).reshape(real, chans)
        x = x + sign_rows(seeds[i], 0, real, frames, pix, chans)
        for j in range(chans // 128):
            natural[j, i * padded : i * padded + real, :] = x[:, j * 128 : (j + 1) * 128]
            natural[j, i * padded + real : (i + 1) * padded, :] = jnp.zeros((padded - real, 128), jnp.float32)
    for f in range(frames):
        for j in range(chans // 128):
            lhs[f * block : (f + 1) * block, j * 128 : (j + 1) * 128] = natural[
                j, pl.ds(f, block, stride=frames), :
            ].astype(jnp.bfloat16)
    copies[1 + clip_dev].wait()
    cap = captions[...].astype(jnp.float32)
    cap = cap / jnp.sqrt(jnp.sum(cap * cap, axis=1, keepdims=True) + 1e-06)
    joined[0:caps_dev, :] = cap
    rest = (frames - 1) * block
    copies[2 + clip_dev].wait()
    pre[...] = jnp.dot(lhs[...], weight[1], preferred_element_type=jnp.float32)
    copies[3 + clip_dev].wait()
    pre[block:, :] += jnp.dot(lhs[0:rest, :], weight[0], preferred_element_type=jnp.float32)
    copies[4 + clip_dev].wait()
    pre[0:rest, :] += jnp.dot(lhs[block:, :], weight[2], preferred_element_type=jnp.float32)
    active = jnp.zeros((block, chans), jnp.float32)
    for f in range(frames):
        v = pre[f * block : (f + 1) * block, :]
        active = active + v * (0.5 + 0.5 * jnp.tanh(GELU_A * v * (1.0 + GELU_B * (v * v))))
    line = lax.broadcasted_iota(jnp.int32, (8, block), 0) % clip_dev
    belongs = (clip_of((8, block), 1, slot, clip_dev) == line).astype(jnp.float32)
    pooled = (exact_dot(belongs, active) * (1.0 / real)).astype(jnp.bfloat16)
    copies[5 + clip_dev].wait()
    video = jnp.dot(pooled, proj[...], preferred_element_type=jnp.float32)
    vnorm = jnp.sqrt(jnp.sum(video * video, axis=1, keepdims=True) + 1e-06)
    vunit = video / vnorm
    unit[0:8, :] = vunit
    unit[8:16, :] = jnp.broadcast_to(vnorm, vunit.shape)
    joined[caps_dev : caps_dev + clip_dev, :] = vunit[0:clip_dev]
    pack[...] = joined[...].astype(jnp.bfloat16)


def slope_kernel(pre, slope):
    v = pre[...]
    square = v * v
    t = jnp.tanh(GELU_A * v * (1.0 + GELU_B * square))
    inner = GELU_A * (1.0 + 3.0 * GELU_B * square)
    slope[...] = (0.5 + 0.5 * t + 0.5 * v * (1.0 - t * t) * inner).astype(jnp.bfloat16)


def backward_kernel(
    dims, seeds, rows, every, unit, slope, weight, proj, out_hbm, loss, out, lhs, acc, natural, colsum, sems,
):
    clip_dev, frames, pix, chans, slot, caps_dev = dims
    real, padded, block = frames * pix, frames * slot, clip_dev * slot
    group = caps_dev + clip_dev
    wide = every.shape[0]
    step = 16 * group
    colsum[...] = jnp.zeros_like(colsum)

    def part(b, carry):
        chunk = every[pl.ds(pl.multiple_of(b * step, step), step), :]
        s = lax.dot_general(chunk, every[...], (((1,), (1,)), ((), ())), preferred_element_type=jnp.float32)
        row = lax.broadcasted_iota(jnp.int32, (step, 1), 0) % group
        colsum[...] += jnp.sum(jnp.where(row >= caps_dev, jnp.exp(s * INV_TEMP), 0.0), axis=0, keepdims=True)
        return carry

    lax.fori_loop(0, wide // step, part, 0)
    mine = every[group - 8 : group, :]
    scores = lax.dot_general(mine, every[...], (((1,), (1,)), ((), ())), preferred_element_type=jnp.float32) * INV_TEMP
    column = lax.broadcasted_iota(jnp.int32, (1, wide), 1)
    line = lax.broadcasted_iota(jnp.int32, (8, 1), 0)
    expo = jnp.where(column % group < caps_dev, jnp.exp(scores), 0.0)
    own = jnp.zeros((8, wide), jnp.float32)
    for i in range(clip_dev):
        for c in range(rows.shape[1]):
            local = lax.rem(rows[i, c], caps_dev)
            own = own + jnp.where((line == 8 - clip_dev + i) & (column == local), 1.0, 0.0)
    sums = colsum[...]
    sums = jnp.where(column % group < caps_dev, sums, 1.0)
    total = jnp.sum(expo, axis=1, keepdims=True)
    owned = own * expo
    positive = jnp.sum(owned, axis=1, keepdims=True)
    text = jnp.sum(own * (jnp.log(sums) - scores), axis=1, keepdims=True)
    safe = jnp.where(line >= 8 - clip_dev, positive, 1.0)
    value = jnp.log(total) - jnp.log(safe) + 0.2 * text
    place = lax.broadcasted_iota(jnp.int32, (8, 128), 1) + (8 - clip_dev)
    picked = jnp.sum(jnp.where(place == line, value, 0.0), axis=0, keepdims=True)
    loss[...] = picked[:, 0:clip_dev]
    coef = expo / total - owned / safe + 0.2 * (expo / sums - own)
    grad = INV_TEMP * jnp.dot(coef.astype(jnp.bfloat16), every[...], preferred_element_type=jnp.float32)
    vunit = unit[0:8, :]
    vnorm = unit[8:16, :]
    grad_video = ((grad - vunit * jnp.sum(vunit * grad, axis=1, keepdims=True)) / vnorm).astype(jnp.bfloat16)
    grad_pooled = lax.dot_general(
        grad_video, proj[...], (((1,), (1,)), ((), ())), preferred_element_type=jnp.float32
    ) * (1.0 / real)
    line = lax.broadcasted_iota(jnp.int32, (block, 8), 1) - (8 - clip_dev)
    belongs = (clip_of((block, 8), 0, slot, clip_dev) == line).astype(jnp.float32)
    spread = exact_dot(belongs, grad_pooled)
    for f in range(frames):
        part = slice(f * block, (f + 1) * block)
        lhs[part, :] = (slope[part, :].astype(jnp.float32) * spread).astype(jnp.bfloat16)
    rest = (frames - 1) * block
    turned = (((1,), (1,)), ((), ()))
    acc[...] = lax.dot_general(lhs[...], weight[1], turned, preferred_element_type=jnp.float32)
    acc[0:rest, :] += lax.dot_general(lhs[block:, :], weight[0], turned, preferred_element_type=jnp.float32)
    acc[block:, :] += lax.dot_general(lhs[0:rest, :], weight[2], turned, preferred_element_type=jnp.float32)
    squares = jnp.zeros((block, chans), jnp.float32)
    for f in range(frames):
        v = acc[f * block : (f + 1) * block, :]
        squares = squares + v * v
    squares = jnp.sum(squares, axis=1, keepdims=True)
    clip = clip_of((block, 1), 0, slot, clip_dev)
    scale = jnp.zeros((block, 1), jnp.float32)
    for i in range(clip_dev):
        mean = jnp.sum(jnp.where(clip == i, squares, 0.0), axis=0, keepdims=True) * (1.0 / (real * chans))
        scale = jnp.where(clip == i, lax.rsqrt(mean + 1e-06), scale)
    for f in range(frames):
        for j in range(chans // 128):
            part = acc[f * block : (f + 1) * block, j * 128 : (j + 1) * 128]
            natural[j, pl.ds(f, block, stride=frames), :] = part * scale
    copies = []
    for i in range(clip_dev):
        rows_i = slice(i * padded, i * padded + real)
        delta = jnp.concatenate([natural[j, rows_i, :] for j in range(chans // 128)], 1)
        delta = delta + sign_rows(seeds[i], 0, real, frames, pix, chans)
        out[i] = delta.reshape(pix, frames, chans).astype(jnp.bfloat16)
        copies.append(pltpu.make_async_copy(out.at[i], out_hbm.at[i], sems.at[i]))
        copies[-1].start()
    for copy in copies:
        copy.wait()


def exchange(pack, blocks):
    held = pack
    steps = []
    step = blocks // 2
    while step:
        steps.append((step,))
        step //= 2
    if blocks == 16:
        steps = [(8,), (6, 4, 2), (1,)]
    for group in steps:
        parts = [lax.ppermute(held, "dp", [(i, i ^ step) for i in range(blocks)]) for step in group]
        held = jnp.concatenate([held] + parts, 0)
    return held


def shards(blocks, clips, sign_seeds, time_weight, proj_weight, captions, caption_rows):
    clip_dev, frames, pix, chans = clips.shape
    caps_dev, embed = captions.shape
    slot = pix + 1
    total = clip_dev * frames * slot
    group = caps_dev + clip_dev
    vmem = pl.BlockSpec(memory_space=pltpu.VMEM)
    smem = pl.BlockSpec(memory_space=pltpu.SMEM)
    hbm = pl.BlockSpec(memory_space=pltpu.HBM)
    params = pltpu.CompilerParams(vmem_limit_bytes=VMEM_LIMIT)
    pack, unit, pre = pl.pallas_call(
        functools.partial(forward_kernel, (clip_dev, frames, pix, chans, slot)),
        out_shape=(
            jax.ShapeDtypeStruct((group, embed), jnp.bfloat16),
            jax.ShapeDtypeStruct((16, embed), jnp.float32),
            jax.ShapeDtypeStruct((total, chans), jnp.float32),
        ),
        in_specs=[hbm] * 5,
        out_specs=(vmem, vmem, vmem),
        scratch_shapes=[
            pltpu.SMEM((clip_dev,), jnp.int32),
            pltpu.VMEM((clip_dev, pix, frames, chans), jnp.bfloat16),
            pltpu.VMEM((3, chans, chans), jnp.bfloat16),
            pltpu.VMEM((chans, embed), jnp.bfloat16),
            pltpu.VMEM((caps_dev, embed), jnp.bfloat16),
            pltpu.VMEM((chans // 128, total, 128), jnp.float32),
            pltpu.VMEM((total, chans), jnp.bfloat16),
            pltpu.VMEM((group, embed), jnp.float32),
            pltpu.SemaphoreType.DMA((6 + clip_dev,)),
        ],
        compiler_params=params,
        cost_estimate=pl.CostEstimate(flops=6 * total * chans * chans, bytes_accessed=14 << 20, transcendentals=total * chans),
        name="forward",
    )(*[
        pltpu.with_memory_space_constraint(operand, pltpu.HBM)
        for operand in (sign_seeds, clips.transpose(0, 2, 1, 3), time_weight, proj_weight, captions)
    ])
    slope = pl.pallas_call(
        slope_kernel,
        out_shape=jax.ShapeDtypeStruct((total, chans), jnp.bfloat16),
        in_specs=[vmem],
        out_specs=vmem,
        compiler_params=pltpu.CompilerParams(vmem_limit_bytes=SLOPE_LIMIT),
        cost_estimate=pl.CostEstimate(flops=16 * total * chans, bytes_accessed=6 * total * chans, transcendentals=total * chans),
        name="slope",
    )(pre)
    every = exchange(pack, blocks)
    delta, loss = pl.pallas_call(
        functools.partial(backward_kernel, (clip_dev, frames, pix, chans, slot, caps_dev)),
        out_shape=(
            jax.ShapeDtypeStruct((clip_dev, pix, frames, chans), jnp.bfloat16),
            jax.ShapeDtypeStruct((1, clip_dev), jnp.float32),
        ),
        in_specs=[smem, smem, vmem, vmem, vmem, vmem, vmem],
        out_specs=(hbm, vmem),
        scratch_shapes=[
            pltpu.VMEM((clip_dev, pix, frames, chans), jnp.bfloat16),
            pltpu.VMEM((total, chans), jnp.bfloat16),
            pltpu.VMEM((total, chans), jnp.float32),
            pltpu.VMEM((chans // 128, total, 128), jnp.float32),
            pltpu.VMEM((1, blocks * group), jnp.float32),
            pltpu.SemaphoreType.DMA((clip_dev,)),
        ],
        compiler_params=params,
        name="backward",
    )(sign_seeds, caption_rows, every, unit, slope, time_weight, proj_weight)
    return delta.transpose(0, 2, 1, 3), loss.reshape(clip_dev)


def solution(mesh):
    in_specs = (
        P(("groups", "dp"), None, None, None),
        P(("groups", "dp")),
        P(),
        P(),
        P(("groups", "dp"), None),
        P(("groups", "dp"), None),
    )
    out_specs = (P(("groups", "dp"), None, None, None), P(("groups", "dp")))
    return jax.shard_map(
        functools.partial(shards, mesh.shape["dp"]),
        mesh=mesh,
        in_specs=in_specs,
        out_specs=out_specs,
        check_vma=False,
    )
```

time: 47.2 us -> 36.4 us (0.77)
  Pallas kernels: 25.9 us -> 21.8 us
  local copies, waits for them, and re-layouts: 4.07 us -> 0.07 us
  waiting for transfers between devices: 8.03 us -> 5.76 us
    pallas_call x1, Pallas kernels: 14.9 us -> 10.4 us  [shards(): pl.pallas_call(functools.partial(backward_kernel, (clip_dev, frames, pix,...]
    unnamed x16 -> x12, local copies, waits for them, and re-layouts: 4.06 us -> 0.05 us
    ppermute x4 -> x5, waiting for transfers between devices: 8.03 us -> 5.76 us  [exchange(): lax.ppermute(held, 'dp', [(i, i ^ step) for i in range(blocks)])]
    pallas_call x0 -> x1, Pallas kernels: none -> 1.85 us  [shards(): pl.pallas_call(slope_kernel, out_shape=jax.ShapeDtypeStruct((total, chans...]
    pallas_call x1, Pallas kernels: 11 us -> 9.59 us  [shards(): pl.pallas_call(functools.partial(forward_kernel, (clip_dev, frames, pix,...]
    ppermute x4 -> x5, starting transfers between devices: 8.12 us -> 7.67 us  [exchange(): lax.ppermute(held, 'dp', [(i, i ^ step) for i in range(blocks)])]
  transfers between devices with their start and end apart: 4 -> 5, of which waited for: 4 -> 3; matrix products, arithmetic and copies ran while one was open for 0% -> 0% of each run, Pallas kernels for 0% -> 5%
where the time goes in v2:
time: 36.4 us; the launch traced here: 36.2 us
  Pallas kernels  21.8 us (60%)
  starting transfers between devices  7.67 us (21%)
  waiting for transfers between devices  5.76 us (16%)
  between operations  0.92 us (3%)
    pallas_call x1, Pallas kernels, shards(): pl.pallas_call(functools.partial(backward_kernel, (clip_dev, frames, pix,...  10.4 us
    pallas_call x1, Pallas kernels, shards(): pl.pallas_call(functools.partial(forward_kernel, (clip_dev, frames, pix,...  9.59 us
    ppermute x5, starting transfers between devices, exchange(): lax.ppermute(held, 'dp', [(i, i ^ step) for i in range(blocks)])  7.67 us
    ppermute x5, waiting for transfers between devices, exchange(): lax.ppermute(held, 'dp', [(i, i ^ step) for i in range(blocks)])  5.76 us
    pallas_call x1, Pallas kernels, shards(): pl.pallas_call(slope_kernel, out_shape=jax.ShapeDtypeStruct((total, chans...  1.85 us
  transfers between devices with their start and end apart: 5, of which 3 were waited for; matrix products, arithmetic and copies ran while one was open for 0% of the time, Pallas kernels for 5%

profile of v2, /device:TPU:0, one launch (start us, length us, event | category | flops | bytes accessed | tf_op | source)
XLA Modules:
  0.0 36.2 jit_solution(8194952587349087955)
XLA Ops:
  0.6 0.0 copy-start
  0.6 9.6 %forward.1 = (bf16[24,512]{1,0:T(8,128)(2,1)S(1)}, f32[16,512]{1,0:T(8,128)S(1)}, f32[800,1024]{1,0:T(8,128)S(1)}) custom-call(s32[4]{0:T(128)} %seeds.1, bf16[4,49,4,1024]{3,2,1,0:T(4,128)(2,1)} %bitcast.3, bf16[3,1024,1024]{2,1,0:T(8,128)(2,1)} %weight.1, bf16[1024,512]{1,0:T(8,128)(2,1)} %proj.1, bf16[20,512]{1,0:T(8,128)(2,1)} %captions_hbm.1), custom_call_target="tpu_custom_call" | custom-call | flops 5033164800 | bytes 14680064 | tf_op jit(solution)/shard_map/forward/pallas_call | solution.py:211
  10.2 4.1 %collective-permute-start = (bf16[24,512]{1,0:T(8,128)(2,1)S(1)}, bf16[24,512]{1,0:T(8,128)(2,1)S(1)}, u32[]{:S(2)}, u32[]{:S(2)}) collective-permute-start(bf16[24,512]{1,0:T(8,128)(2,1)S(1)} %get-tuple-element.7), channel_id=1, source_target_pairs={{0,8},{1,9},{2,10},{3,11},{4,12},{5,13},{6,14},{7,15},{8,0},{9,1},... | collective-permute-start | bytes 73736 | tf_op jit(solution)/shard_map/ppermute | solution.py:196
  14.4 1.8 %collective-permute-done = bf16[24,512]{1,0:T(8,128)(2,1)S(1)} collective-permute-done((bf16[24,512]{1,0:T(8,128)(2,1)S(1)}, bf16[24,512]{1,0:T(8,128)(2,1)S(1)}, u32[]{:S(2)}, u32[]{:S(2)}) %collective-permute-start) | collective-permute-done | bytes 24608 | tf_op jit(solution)/shard_map/ppermute | solution.py:196
  16.2 2.8 %collective-permute-start.1 = (bf16[48,512]{1,0:T(8,128)(2,1)S(1)}, bf16[48,512]{1,0:T(8,128)(2,1)S(1)}, u32[]{:S(2)}, u32[]{:S(2)}) collective-permute-start(bf16[48,512]{1,0:T(8,128)(2,1)S(1)} %get-tuple-element.20), channel_id=1, source_target_pairs={{0,6},{1,7},{2,4},{3,5},{4,2},{5,3},{6,0},{7,1},{8,14},{9,15},{10,... | collective-permute-start | bytes 147464 | tf_op jit(solution)/shard_map/ppermute | solution.py:196
  19.0 0.5 %collective-permute-start.3 = (bf16[48,512]{1,0:T(8,128)(2,1)S(1)}, bf16[48,512]{1,0:T(8,128)(2,1)S(1)}, u32[]{:S(2)}, u32[]{:S(2)}) collective-permute-start(bf16[48,512]{1,0:T(8,128)(2,1)S(1)} %get-tuple-element.20), channel_id=1, source_target_pairs={{0,2},{1,3},{2,0},{3,1},{4,6},{5,7},{6,4},{7,5},{8,10},{9,11},{10,... | collective-permute-start | bytes 147464 | tf_op jit(solution)/shard_map/ppermute | solution.py:196
  19.5 0.1 collective-permute-start.2
  19.7 1.5 %collective-permute-done.1 = bf16[48,512]{1,0:T(8,128)(2,1)S(1)} collective-permute-done((bf16[48,512]{1,0:T(8,128)(2,1)S(1)}, bf16[48,512]{1,0:T(8,128)(2,1)S(1)}, u32[]{:S(2)}, u32[]{:S(2)}) %collective-permute-start.1) | collective-permute-done | bytes 49184 | tf_op jit(solution)/shard_map/ppermute | solution.py:196
  21.2 2.4 %collective-permute-done.2 = bf16[48,512]{1,0:T(8,128)(2,1)S(1)} collective-permute-done((bf16[48,512]{1,0:T(8,128)(2,1)S(1)}, bf16[48,512]{1,0:T(8,128)(2,1)S(1)}, u32[]{:S(2)}, u32[]{:S(2)}) %collective-permute-start.2) | collective-permute-done | bytes 49184 | tf_op jit(solution)/shard_map/ppermute | solution.py:196
  23.6 0.0 collective-permute-done.3
  23.7 0.1 collective-permute-start.4
  23.7 0.0 copy-start.1
  23.7 0.0 copy-start.2
  23.8 0.0 copy-start.3
  23.8 1.9 %slope.1 = bf16[800,1024]{1,0:T(8,128)(2,1)S(1)} custom-call(f32[800,1024]{1,0:T(8,128)S(1)} %get-tuple-element.9.pre), custom_call_target="tpu_custom_call" | custom-call | flops 13107200 | bytes 4915200 | tf_op jit(solution)/shard_map/slope/pallas_call | solution.py:238
  25.6 0.0 collective-permute-done.4
  25.7 0.0 copy-done
  25.7 0.0 copy-done.1
  25.7 0.0 copy-done.2
  25.7 0.0 copy-done.3
  25.7 10.4 %backward.1 = (bf16[4,49,4,1024]{3,2,1,0:T(4,128)(2,1)}, f32[1,4]{1,0:T(1,128)}) custom-call(s32[4]{0:T(128)S(1)} %copy-done.3, s32[4,5]{1,0:T(4,128)S(1)} %copy-done.2, bf16[384,512]{1,0:T(8,128)(2,1)S(1)} %constant_dynamic-update-slice_fusion.7.every, f32[16,512]{1,0:T(8,128)S(1)} %get-tuple-element.8.unit, bf16[800,1024]{1,0:T(8,128)(2,1)S(1)} %slope.1, ...), custom_call_target="tpu_custom_call" | custom-call | tf_op jit(solution)/shard_map/backward/pallas_call | solution.py:248
  (6 shorter events, 0.1 us)
Async XLA Ops:
  0.6 25.0 %copy-start = (bf16[3,1024,1024]{2,1,0:T(8,128)(2,1)S(1)}, bf16[3,1024,1024]{2,1,0:T(8,128)(2,1)}, u32[]{:S(2)}) copy-start(bf16[3,1024,1024]{2,1,0:T(8,128)(2,1)} %weight.1) | copy-start | bytes 18874372
  10.2 5.9 %collective-permute-start = (bf16[24,512]{1,0:T(8,128)(2,1)S(1)}, bf16[24,512]{1,0:T(8,128)(2,1)S(1)}, u32[]{:S(2)}, u32[]{:S(2)}) collective-permute-start(bf16[24,512]{1,0:T(8,128)(2,1)S(1)} %get-tuple-element.7), channel_id=1, source_target_pairs={{0,8},{1,9},{2,10},{3,11},{4,12},{5,13},{6,14},{7,15},{8,0},{9,1},... | collective-permute-start | bytes 73736 | tf_op jit(solution)/shard_map/ppermute | solution.py:196
  16.2 5.0 %collective-permute-start.1 = (bf16[48,512]{1,0:T(8,128)(2,1)S(1)}, bf16[48,512]{1,0:T(8,128)(2,1)S(1)}, u32[]{:S(2)}, u32[]{:S(2)}) collective-permute-start(bf16[48,512]{1,0:T(8,128)(2,1)S(1)} %get-tuple-element.20), channel_id=1, source_target_pairs={{0,6},{1,7},{2,4},{3,5},{4,2},{5,3},{6,0},{7,1},{8,14},{9,15},{10,... | collective-permute-start | bytes 147464 | tf_op jit(solution)/shard_map/ppermute | solution.py:196
  19.0 4.6 %collective-permute-start.3 = (bf16[48,512]{1,0:T(8,128)(2,1)S(1)}, bf16[48,512]{1,0:T(8,128)(2,1)S(1)}, u32[]{:S(2)}, u32[]{:S(2)}) collective-permute-start(bf16[48,512]{1,0:T(8,128)(2,1)S(1)} %get-tuple-element.20), channel_id=1, source_target_pairs={{0,2},{1,3},{2,0},{3,1},{4,6},{5,7},{6,4},{7,5},{8,10},{9,11},{10,... | collective-permute-start | bytes 147464 | tf_op jit(solution)/shard_map/ppermute | solution.py:196
  19.5 4.1 %collective-permute-start.2 = (bf16[48,512]{1,0:T(8,128)(2,1)S(1)}, bf16[48,512]{1,0:T(8,128)(2,1)S(1)}, u32[]{:S(2)}, u32[]{:S(2)}) collective-permute-start(bf16[48,512]{1,0:T(8,128)(2,1)S(1)} %get-tuple-element.20), channel_id=1, source_target_pairs={{0,4},{1,5},{2,6},{3,7},{4,0},{5,1},{6,2},{7,3},{8,12},{9,13},{10,... | collective-permute-start | bytes 147464 | tf_op jit(solution)/shard_map/ppermute | solution.py:196
  23.7 2.0 %collective-permute-start.4 = (bf16[192,512]{1,0:T(8,128)(2,1)S(1)}, bf16[192,512]{1,0:T(8,128)(2,1)S(1)}, u32[]{:S(2)}, u32[]{:S(2)}) collective-permute-start(bf16[192,512]{1,0:T(8,128)(2,1)S(1)} %get-tuple-element.12), channel_id=1, source_target_pairs={{0,1},{1,0},{2,3},{3,2},{4,5},{5,4},{6,7},{7,6},{8,9},{9,8},{10,11... | collective-permute-start | bytes 589832 | tf_op jit(solution)/shard_map/ppermute | solution.py:196
  23.7 1.9 %copy-start.1 = (bf16[1024,512]{1,0:T(8,128)(2,1)S(1)}, bf16[1024,512]{1,0:T(8,128)(2,1)}, u32[]{:S(2)}) copy-start(bf16[1024,512]{1,0:T(8,128)(2,1)} %proj.1) | copy-start | bytes 3145732
  23.7 1.9 %copy-start.2 = (s32[4,5]{1,0:T(4,128)S(1)}, s32[4,5]{1,0:T(4,128)}, u32[]{:S(2)}) copy-start(s32[4,5]{1,0:T(4,128)} %rows.1) | copy-start | bytes 244
  23.8 1.9 %copy-start.3 = (s32[4]{0:T(128)S(1)}, s32[4]{0:T(128)}, u32[]{:S(2)}) copy-start(s32[4]{0:T(128)} %seeds.1) | copy-start | bytes 52

commit v3 on v2

v3 whole, which is shorter than its diff:
```python
import functools

import jax
import jax.numpy as jnp
from jax import lax
from jax.experimental import pallas as pl
from jax.experimental.pallas import tpu as pltpu
from jax.sharding import PartitionSpec as P

INV_TEMP = 1.0 / 0.07
GELU_A = 0.7978845608028654
GELU_B = 0.044715
LANES = 128
CHUNK = 256
HASH_STEP = 374761393
HASH_SEED = -1640531535
HASH_MIX = 668265263


def wrap(value):
    return jnp.int32((value + 2**31) % 2**32 - 2**31)


def signs(mixed):
    mixed = mixed ^ (mixed >> 13)
    mixed = mixed * jnp.int32(HASH_MIX)
    mixed = mixed ^ (mixed >> 16)
    return jnp.where((mixed & 128) != 0, jnp.float32(0.1), jnp.float32(-0.1))


def clip_of(shape, dim, pix, clip_dev):
    return lax.broadcasted_iota(jnp.int32, shape, dim) // pix


def forward_kernel(
    dims, seeds_hbm, rows_hbm, clips_hbm, weight_hbm, proj_hbm, captions_hbm,
    pack, unit, pre, start, own, weight, proj,
    seeds, rows, clips, captions, natural, lhs, active, joined, clip_sems, weight_sems, sems,
):
    clip_dev, frames, pix, chans, block = dims
    dense, tiles = clip_dev * pix, chans // LANES
    caps_dev = captions.shape[0]
    per_chunk = CHUNK // LANES
    small = [
        pltpu.make_async_copy(src, dst, sems.at[i])
        for i, (src, dst) in enumerate(
            [(seeds_hbm, seeds), (rows_hbm, rows), (captions_hbm, captions), (proj_hbm, proj)]
        )
    ]
    clip_copies = [
        pltpu.make_async_copy(clips_hbm.at[:, :, j * LANES : (j + 1) * LANES], clips.at[j], clip_sems.at[j])
        for j in range(tiles)
    ]
    weight_copies = [
        pltpu.make_async_copy(
            weight_hbm.at[:, k * CHUNK : (k + 1) * CHUNK, :],
            weight.at[:, k * CHUNK : (k + 1) * CHUNK, :],
            weight_sems.at[k],
        )
        for k in range(chans // CHUNK)
    ]
    chunks = chans // CHUNK

    def fetch(k):
        for copy in clip_copies[k * per_chunk : (k + 1) * per_chunk]:
            copy.start()
        weight_copies[k].start()

    small[0].start()
    fetch(0)
    for copy in small[1:3]:
        copy.start()
    fetch(1)
    for f in range(frames):
        lhs[f * block + dense : (f + 1) * block, :] = jnp.zeros((block - dense, chans), jnp.bfloat16)
    row = lax.broadcasted_iota(jnp.int32, (dense * frames, LANES), 0)
    spot = row // frames
    clip = spot // pix
    first = ((row % frames) * pix + spot - clip * pix) * chans + lax.broadcasted_iota(jnp.int32, row.shape, 1)
    small[0].wait()
    seed = jnp.zeros(row.shape, jnp.int32)
    for i in range(clip_dev):
        seed = jnp.where(clip == i, seeds[i], seed)
    start[...] = seed * jnp.int32(HASH_SEED) + first * jnp.int32(HASH_STEP)

    def hash_piece(j, rows):
        def run():
            x = clips[j, rows.start // frames : rows.stop // frames].reshape(rows.stop - rows.start, LANES)
            natural[j, rows, :] = x.astype(jnp.float32) + signs(start[rows, :] + wrap(j * LANES * HASH_STEP))

        return run

    def order_piece(j, f):
        def run():
            lhs[f * block : f * block + dense, j * LANES : (j + 1) * LANES] = natural[
                j, pl.ds(f, dense, stride=frames), :
            ].astype(jnp.bfloat16)

        return run

    def prepare(k):
        mine = range(k * per_chunk, (k + 1) * per_chunk)
        for j in mine:
            clip_copies[j].wait()
        length = dense * frames
        cut = next(c for c in (112, 56, 16, length) if length % c == 0)
        pieces = [hash_piece(j, slice(r, r + cut)) for j in mine for r in range(0, length, cut)]
        return pieces + [order_piece(j, f) for j in mine for f in range(frames)]

    def activate(f, columns):
        def run():
            v = pre[f * block : (f + 1) * block, columns]
            gelu = v * (0.5 + 0.5 * jnp.tanh(GELU_A * v * (1.0 + GELU_B * (v * v))))
            active[:, columns] = gelu if f == 0 else active[:, columns] + gelu

        return run

    for piece in prepare(0):
        piece()
    small[1].wait()
    small[2].wait()
    places = [(i, c) for i in range(clip_dev) for c in range(rows.shape[1])]
    base = rows[0, 0]
    for i, c in places:
        base = jnp.minimum(base, rows[i, c])
    line = lax.broadcasted_iota(jnp.int32, own.shape, 0)
    column = lax.broadcasted_iota(jnp.int32, own.shape, 1) + base
    mine = jnp.zeros(own.shape, jnp.float32)
    for i, c in places:
        mine = jnp.where((line == 8 - clip_dev + i) & (column == rows[i, c]), 1.0, mine)
    own[...] = mine
    cap = captions[...].astype(jnp.float32)
    cap = cap / jnp.sqrt(jnp.sum(cap * cap, axis=1, keepdims=True) + 1e-06)
    joined[0:caps_dev, :] = cap
    late = []
    for k in range(chunks):
        weight_copies[k].wait()
        if k + 2 < chunks:
            fetch(k + 2)
        elif k + 2 == chunks:
            small[3].start()
        pieces = prepare(k + 1) if k + 1 < chunks else []
        part = slice(k * CHUNK, (k + 1) * CHUNK)
        products = [(f, n) for n in range(chunks) for f in range(frames)]
        for count, (f, n) in enumerate(products):
            columns = slice(n * CHUNK, (n + 1) * CHUNK)
            taps = [t for t in range(3) if 0 <= f + t - 1 < frames]
            left = jnp.concatenate([lhs[(f + t - 1) * block : (f + t) * block, part] for t in taps], 1)
            right = jnp.concatenate([weight[t, part, columns] for t in taps], 0)
            v = jnp.dot(left, right, preferred_element_type=jnp.float32)
            if k:
                v = v + pre[f * block : (f + 1) * block, columns]
            pre[f * block : (f + 1) * block, columns] = v
            done, todo = len(pieces) * count // len(products), len(pieces) * (count + 1) // len(products)
            for piece in pieces[done:todo]:
                piece()
            if k + 1 == chunks:
                late.append(activate(f, columns))
                if len(late) > 1:
                    late.pop(0)()
    for piece in late:
        piece()
    sums = []
    for i in range(clip_dev):
        low, high = i * pix // 8 * 8, min(-(-(i + 1) * pix // 8) * 8, block)
        row = lax.broadcasted_iota(jnp.int32, (high - low, 1), 0) + low
        inside = (row >= i * pix) & (row < (i + 1) * pix)
        sums.append(jnp.sum(jnp.where(inside, active[low:high, :], 0.0), axis=0, keepdims=True))
    pooled = (jnp.concatenate(sums + sums, 0) * (1.0 / (frames * pix))).astype(jnp.bfloat16)
    small[3].wait()
    video = jnp.dot(pooled, proj[...], preferred_element_type=jnp.float32)
    vnorm = jnp.sqrt(jnp.sum(video * video, axis=1, keepdims=True) + 1e-06)
    vunit = video / vnorm
    unit[0:8, :] = vunit
    unit[8:16, :] = jnp.broadcast_to(vnorm, vunit.shape)
    joined[caps_dev : caps_dev + clip_dev, :] = vunit[0:clip_dev]
    pack[...] = joined[...].astype(jnp.bfloat16)


def slope_kernel(pre, slope):
    v = pre[...]
    square = v * v
    t = jnp.tanh(GELU_A * v * (1.0 + GELU_B * square))
    inner = GELU_A * (1.0 + 3.0 * GELU_B * square)
    slope[...] = (0.5 + 0.5 * t + 0.5 * v * (1.0 - t * t) * inner).astype(jnp.bfloat16)


def delta_kernel(start, delta):
    for j in range(delta.shape[0]):
        delta[j] = signs(start[...] + wrap(j * LANES * HASH_STEP))


def backward_kernel(
    dims, every, unit, own, slope, delta, weight, proj, out_hbm, loss,
    out, lhs, acc, natural, colsum, sems,
):
    clip_dev, frames, pix, chans, block, caps_dev = dims
    dense, tiles = clip_dev * pix, chans // LANES
    real = frames * pix
    group = caps_dev + clip_dev
    wide = every.shape[0]
    step = 16 * group
    colsum[...] = jnp.zeros_like(colsum)

    def part(b, carry):
        chunk = every[pl.ds(pl.multiple_of(b * step, step), step), :]
        s = lax.dot_general(chunk, every[...], (((1,), (1,)), ((), ())), preferred_element_type=jnp.float32)
        row = lax.broadcasted_iota(jnp.int32, (step, 1), 0) % group
        colsum[...] += jnp.sum(jnp.where(row >= caps_dev, jnp.exp(s * INV_TEMP), 0.0), axis=0, keepdims=True)
        return carry

    lax.fori_loop(0, wide // step, part, 0)
    mine = every[group - 8 : group, :]
    scores = lax.dot_general(mine, every[...], (((1,), (1,)), ((), ())), preferred_element_type=jnp.float32) * INV_TEMP
    column = lax.broadcasted_iota(jnp.int32, (1, wide), 1)
    line = lax.broadcasted_iota(jnp.int32, (8, 1), 0)
    expo = jnp.where(column % group < caps_dev, jnp.exp(scores), 0.0)
    owns = jnp.concatenate([own[...], jnp.zeros((8, wide - own.shape[1]), jnp.float32)], 1)
    sums = jnp.where(column % group < caps_dev, colsum[...], 1.0)
    total = jnp.sum(expo, axis=1, keepdims=True)
    owned = owns * expo
    positive = jnp.sum(owned, axis=1, keepdims=True)
    text = jnp.sum(owns * (jnp.log(sums) - scores), axis=1, keepdims=True)
    safe = jnp.where(line >= 8 - clip_dev, positive, 1.0)
    value = jnp.log(total) - jnp.log(safe) + 0.2 * text
    place = lax.broadcasted_iota(jnp.int32, (8, LANES), 1) + (8 - clip_dev)
    picked = jnp.sum(jnp.where(place == line, value, 0.0), axis=0, keepdims=True)
    loss[...] = picked[:, 0:clip_dev]
    coef = expo / total - owned / safe + 0.2 * (expo / sums - owns)
    grad = INV_TEMP * jnp.dot(coef.astype(jnp.bfloat16), every[...], preferred_element_type=jnp.float32)
    vunit = unit[0:8, :]
    vnorm = unit[8:16, :]
    grad_video = ((grad - vunit * jnp.sum(vunit * grad, axis=1, keepdims=True)) / vnorm).astype(jnp.bfloat16)
    grad_pooled = lax.dot_general(
        grad_video, proj[...], (((1,), (1,)), ((), ())), preferred_element_type=jnp.float32
    ) * (1.0 / real)
    clip = clip_of((block, 1), 0, pix, clip_dev)
    spread = jnp.zeros((block, chans), jnp.float32)
    for i in range(clip_dev):
        spread = jnp.where(clip == i, grad_pooled[8 - clip_dev + i : 9 - clip_dev + i, :], spread)
    for f in range(frames):
        rows = slice(f * block, (f + 1) * block)
        lhs[rows, :] = (slope[rows, :].astype(jnp.float32) * spread).astype(jnp.bfloat16)
    rest = (frames - 1) * block
    turned = (((1,), (1,)), ((), ()))
    acc[...] = lax.dot_general(lhs[...], weight[1], turned, preferred_element_type=jnp.float32)
    acc[0:rest, :] += lax.dot_general(lhs[block:, :], weight[0], turned, preferred_element_type=jnp.float32)
    acc[block:, :] += lax.dot_general(lhs[0:rest, :], weight[2], turned, preferred_element_type=jnp.float32)
    squares = jnp.zeros((block, chans), jnp.float32)
    for f in range(frames):
        v = acc[f * block : (f + 1) * block, :]
        squares = squares + v * v
    squares = jnp.sum(squares, axis=1, keepdims=True)
    scale = jnp.zeros((block, 1), jnp.float32)
    for i in range(clip_dev):
        mean = jnp.sum(jnp.where(clip == i, squares, 0.0), axis=0, keepdims=True) * (1.0 / (real * chans))
        scale = jnp.where(clip == i, lax.rsqrt(mean + 1e-06), scale)
    scale = jnp.broadcast_to(scale, (block, LANES))[0:dense]
    copies = []
    for j in range(tiles):
        lanes = slice(j * LANES, (j + 1) * LANES)
        for f in range(frames):
            natural[j, pl.ds(f, dense, stride=frames), :] = acc[f * block : f * block + dense, lanes] * scale
        out[j] = (natural[j] + delta[j]).astype(jnp.bfloat16).reshape(dense, frames, LANES)
        copies.append(pltpu.make_async_copy(out.at[j], out_hbm.at[:, :, lanes], sems.at[j]))
        copies[-1].start()
    for copy in copies:
        copy.wait()


def swap(held, blocks, steps):
    parts = [lax.ppermute(held, "dp", [(i, i ^ step) for i in range(blocks)]) for step in steps]
    return jnp.concatenate([held] + parts, 0)


def shards(blocks, clips, sign_seeds, time_weight, proj_weight, captions, caption_rows):
    clip_dev, frames, pix, chans = clips.shape
    caps_dev, embed = captions.shape
    dense = clip_dev * pix
    block = -(-dense // 8) * 8
    total = frames * block
    group = caps_dev + clip_dev
    tiles = chans // LANES
    bf16, f32, i32 = jnp.bfloat16, jnp.float32, jnp.int32
    shape = jax.ShapeDtypeStruct
    vmem = pl.BlockSpec(memory_space=pltpu.VMEM)
    hbm = pl.BlockSpec(memory_space=pltpu.HBM)
    pack, unit, pre, start, own, weight, proj = pl.pallas_call(
        functools.partial(forward_kernel, (clip_dev, frames, pix, chans, block)),
        out_shape=(
            shape((group, embed), bf16),
            shape((16, embed), f32),
            shape((total, chans), f32),
            shape((dense * frames, LANES), i32),
            shape((8, -(-caps_dev // LANES) * LANES), f32),
            shape((3, chans, chans), bf16),
            shape((chans, embed), bf16),
        ),
        in_specs=[hbm] * 6,
        out_specs=(vmem,) * 7,
        scratch_shapes=[
            pltpu.SMEM((clip_dev,), i32),
            pltpu.SMEM(caption_rows.shape, i32),
            pltpu.VMEM((tiles, dense, frames, LANES), bf16),
            pltpu.VMEM((caps_dev, embed), bf16),
            pltpu.VMEM((tiles, dense * frames, LANES), f32),
            pltpu.VMEM((total, chans), bf16),
            pltpu.VMEM((block, chans), f32),
            pltpu.VMEM((group, embed), f32),
            pltpu.SemaphoreType.DMA((tiles,)),
            pltpu.SemaphoreType.DMA((chans // CHUNK,)),
            pltpu.SemaphoreType.DMA((4,)),
        ],
        compiler_params=pltpu.CompilerParams(vmem_limit_bytes=28 << 20),
        name="forward",
    )(*[
        pltpu.with_memory_space_constraint(operand, pltpu.HBM)
        for operand in (
            sign_seeds,
            caption_rows,
            clips.transpose(0, 2, 1, 3).reshape(dense, frames, chans),
            time_weight,
            proj_weight,
            captions,
        )
    ])
    slope = pl.pallas_call(
        slope_kernel,
        out_shape=shape((total, chans), bf16),
        in_specs=[vmem],
        out_specs=vmem,
        compiler_params=pltpu.CompilerParams(vmem_limit_bytes=8 << 20),
        cost_estimate=pl.CostEstimate(flops=16 * total * chans, bytes_accessed=6 * total * chans, transcendentals=total * chans),
        name="slope",
    )(pre)
    delta = pl.pallas_call(
        delta_kernel,
        out_shape=shape((tiles, dense * frames, LANES), f32),
        in_specs=[vmem],
        out_specs=vmem,
        compiler_params=pltpu.CompilerParams(vmem_limit_bytes=8 << 20),
        cost_estimate=pl.CostEstimate(flops=10 * dense * frames * chans, bytes_accessed=4 * dense * frames * chans, transcendentals=0),
        name="delta",
    )(start)
    if blocks == 16:
        rounds = [(8,), (2, 4, 6), (1,)]
    else:
        rounds = [(1 << b,) for b in reversed(range(blocks.bit_length() - 1))]
    every = pack
    for i, steps in enumerate(rounds):
        every = swap(every, blocks, steps)
        if i == 0:
            every, slope = lax.optimization_barrier((every, slope))
        if i == 1:
            every, delta = lax.optimization_barrier((every, delta))
    out, loss = pl.pallas_call(
        functools.partial(backward_kernel, (clip_dev, frames, pix, chans, block, caps_dev)),
        out_shape=(shape((dense, frames, chans), bf16), shape((1, clip_dev), f32)),
        in_specs=[vmem] * 7,
        out_specs=(hbm, vmem),
        scratch_shapes=[
            pltpu.VMEM((tiles, dense, frames, LANES), bf16),
            pltpu.VMEM((total, chans), bf16),
            pltpu.VMEM((total, chans), f32),
            pltpu.VMEM((tiles, dense * frames, LANES), f32),
            pltpu.VMEM((1, blocks * group), f32),
            pltpu.SemaphoreType.DMA((tiles,)),
        ],
        compiler_params=pltpu.CompilerParams(vmem_limit_bytes=24 << 20),
        name="backward",
    )(every, unit, own, slope, delta, weight, proj)
    out = out.reshape(clip_dev, pix, frames, chans).transpose(0, 2, 1, 3)
    return out, loss.reshape(clip_dev)


def solution(mesh):
    in_specs = (
        P(("groups", "dp"), None, None, None),
        P(("groups", "dp")),
        P(),
        P(),
        P(("groups", "dp"), None),
        P(("groups", "dp"), None),
    )
    out_specs = (P(("groups", "dp"), None, None, None), P(("groups", "dp")))
    return jax.shard_map(
        functools.partial(shards, mesh.shape["dp"]),
        mesh=mesh,
        in_specs=in_specs,
        out_specs=out_specs,
        check_vma=False,
    )
```

time: 36.4 us -> 34.4 us (0.945)
  waiting for transfers between devices: 5.76 us -> 4.41 us
  Pallas kernels: 21.8 us -> 21.3 us
    pallas_call x1, Pallas kernels: 10.4 us -> 8.75 us  [shards(): pl.pallas_call(functools.partial(backward_kernel, (clip_dev, frames, pix,...]
    ppermute x5, waiting for transfers between devices: 5.76 us -> 4.41 us  [swap(): lax.ppermute(held, 'dp', [(i, i ^ step) for i in range(blocks)])]
    pallas_call x1 -> x2, Pallas kernels: 1.85 us -> 2.79 us  [the longest x1 1.85 us: shards(): pl.pallas_call(slope_kernel, out_shape=shape((total, chans), bf16), in_sp...]
  transfers between devices with their start and end apart: 5 -> 5, of which waited for: 3 -> 4; matrix products, arithmetic and copies ran while one was open for 0% -> 0% of each run, Pallas kernels for 5% -> 8%
where the time goes in v3:
time: 34.4 us; the launch traced here: 34.3 us
  Pallas kernels  21.3 us (62%)
  starting transfers between devices  7.73 us (22%)
  waiting for transfers between devices  4.41 us (13%)
  between operations  0.84 us (2%)
    pallas_call x1, Pallas kernels, shards(): pl.pallas_call(functools.partial(forward_kernel, (clip_dev, frames, pix,...  9.72 us
    pallas_call x1, Pallas kernels, shards(): pl.pallas_call(functools.partial(backward_kernel, (clip_dev, frames, pix,...  8.75 us
    ppermute x5, starting transfers between devices, swap(): lax.ppermute(held, 'dp', [(i, i ^ step) for i in range(blocks)])  7.73 us
    ppermute x5, waiting for transfers between devices, swap(): lax.ppermute(held, 'dp', [(i, i ^ step) for i in range(blocks)])  4.41 us
    pallas_call x1, Pallas kernels, shards(): pl.pallas_call(slope_kernel, out_shape=shape((total, chans), bf16), in_sp...  1.85 us
    pallas_call x1, Pallas kernels, shards(): pl.pallas_call(delta_kernel, out_shape=shape((tiles, dense * frames, LANE...  0.94 us
  transfers between devices with their start and end apart: 5, of which 4 were waited for; matrix products, arithmetic and copies ran while one was open for 0% of the time, Pallas kernels for 8%

profile of v3, /device:TPU:0, one launch (start us, length us, event | category | flops | bytes accessed | tf_op | source)
XLA Modules:
  0.0 34.3 jit_solution(13602507127180272016)
XLA Ops:
  0.6 9.7 %forward.1 = (bf16[24,512]{1,0:T(8,128)(2,1)S(1)}, f32[16,512]{1,0:T(8,128)S(1)}, f32[800,1024]{1,0:T(8,128)S(1)}, s32[784,128]{1,0:T(8,128)S(1)}, f32[8,128]{1,...) custom-call(s32[4]{0:T(128)} %seeds_hbm.1, s32[4,5]{1,0:T(4,128)} %rows_hbm.1, ...), custom_call_target="tpu_custom_call" | custom-call | tf_op jit(solution)/shard_map/forward/pallas_call | solution.py:288
  10.4 4.1 %collective-permute-start = (bf16[24,512]{1,0:T(8,128)(2,1)S(1)}, bf16[24,512]{1,0:T(8,128)(2,1)S(1)}, u32[]{:S(2)}, u32[]{:S(2)}) collective-permute-start(bf16[24,512]{1,0:T(8,128)(2,1)S(1)} %get-tuple-element.15), channel_id=1, source_target_pairs={{0,8},{1,9},{2,10},{3,11},{4,12},{5,13},{6,14},{7,15},{8,0},{9,1},... | collective-permute-start | bytes 73736 | tf_op jit(solution)/shard_map/ppermute | solution.py:272
  14.5 1.9 %slope.1 = bf16[800,1024]{1,0:T(8,128)(2,1)S(1)} custom-call(f32[800,1024]{1,0:T(8,128)S(1)} %get-tuple-element.16.pre), custom_call_target="tpu_custom_call" | custom-call | flops 13107200 | bytes 4915200 | tf_op jit(solution)/shard_map/slope/pallas_call | solution.py:327
  16.3 0.0 collective-permute-done
  16.3 2.8 %collective-permute-start.3 = (bf16[48,512]{1,0:T(8,128)(2,1)S(1)}, bf16[48,512]{1,0:T(8,128)(2,1)S(1)}, u32[]{:S(2)}, u32[]{:S(2)}) collective-permute-start(bf16[48,512]{1,0:T(8,128)(2,1)S(1)} %pad_maximum_fusion.2), channel_id=1, source_target_pairs={{0,6},{1,7},{2,4},{3,5},{4,2},{5,3},{6,0},{7,1},{8,14},{9,15},{10,... | collective-permute-start | bytes 147464 | tf_op jit(solution)/shard_map/ppermute | solution.py:272
  19.1 0.6 %collective-permute-start.2 = (bf16[48,512]{1,0:T(8,128)(2,1)S(1)}, bf16[48,512]{1,0:T(8,128)(2,1)S(1)}, u32[]{:S(2)}, u32[]{:S(2)}) collective-permute-start(bf16[48,512]{1,0:T(8,128)(2,1)S(1)} %pad_maximum_fusion.2), channel_id=1, source_target_pairs={{0,4},{1,5},{2,6},{3,7},{4,0},{5,1},{6,2},{7,3},{8,12},{9,13},{10,... | collective-permute-start | bytes 147464 | tf_op jit(solution)/shard_map/ppermute | solution.py:272
  19.7 0.2 collective-permute-start.1
  19.9 0.9 %delta.1 = f32[8,784,128]{2,1,0:T(8,128)S(1)} custom-call(s32[784,128]{1,0:T(8,128)S(1)} %get-tuple-element.18.start), custom_call_target="tpu_custom_call" | custom-call | flops 8028160 | bytes 3211264 | tf_op jit(solution)/shard_map/delta/pallas_call | solution.py:336
  20.8 1.1 %collective-permute-done.3 = bf16[48,512]{1,0:T(8,128)(2,1)S(1)} collective-permute-done((bf16[48,512]{1,0:T(8,128)(2,1)S(1)}, bf16[48,512]{1,0:T(8,128)(2,1)S(1)}, u32[]{:S(2)}, u32[]{:S(2)}) %collective-permute-start.3) | collective-permute-done | bytes 49184 | tf_op jit(solution)/shard_map/ppermute | solution.py:272
  21.9 1.3 %collective-permute-done.2 = bf16[48,512]{1,0:T(8,128)(2,1)S(1)} collective-permute-done((bf16[48,512]{1,0:T(8,128)(2,1)S(1)}, bf16[48,512]{1,0:T(8,128)(2,1)S(1)}, u32[]{:S(2)}, u32[]{:S(2)}) %collective-permute-start.2) | collective-permute-done | bytes 49184 | tf_op jit(solution)/shard_map/ppermute | solution.py:272
  23.2 0.6 %collective-permute-done.1 = bf16[48,512]{1,0:T(8,128)(2,1)S(1)} collective-permute-done((bf16[48,512]{1,0:T(8,128)(2,1)S(1)}, bf16[48,512]{1,0:T(8,128)(2,1)S(1)}, u32[]{:S(2)}, u32[]{:S(2)}) %collective-permute-start.1) | collective-permute-done | bytes 49184 | tf_op jit(solution)/shard_map/ppermute | solution.py:272
  23.8 0.1 collective-permute-start.4
  23.9 1.4 %collective-permute-done.4 = bf16[192,512]{1,0:T(8,128)(2,1)S(1)} collective-permute-done((bf16[192,512]{1,0:T(8,128)(2,1)S(1)}, bf16[192,512]{1,0:T(8,128)(2,1)S(1)}, u32[]{:S(2)}, u32[]{:S(2)}) %collective-permute-start.4) | collective-permute-done | bytes 196640 | tf_op jit(solution)/shard_map/ppermute | solution.py:272
  25.4 8.8 %backward.1 = (bf16[196,4,1024]{2,1,0:T(4,128)(2,1)}, f32[1,4]{1,0:T(1,128)}) custom-call(bf16[384,512]{1,0:T(8,128)(2,1)S(1)} %pad_maximum_fusion.every, f32[16,512]{1,0:T(8,128)S(1)} %get-tuple-element.20.unit, f32[8,128]{1,0:T(8,128)S(1)} %get-tuple-element.21.own, bf16[800,1024]{1,0:T(8,128)(2,1)S(1)} %slope.1, f32[8,784,128]{2,1,0:T(8,128)S(1)} %delta.1, ...), custom_call_target="tpu_custom_call" | custom-call | tf_op jit(solution)/shard_map/backward/pallas_call | solution.py:356
  (3 shorter events, 0.0 us)
Async XLA Ops:
  10.4 6.0 %collective-permute-start = (bf16[24,512]{1,0:T(8,128)(2,1)S(1)}, bf16[24,512]{1,0:T(8,128)(2,1)S(1)}, u32[]{:S(2)}, u32[]{:S(2)}) collective-permute-start(bf16[24,512]{1,0:T(8,128)(2,1)S(1)} %get-tuple-element.15), channel_id=1, source_target_pairs={{0,8},{1,9},{2,10},{3,11},{4,12},{5,13},{6,14},{7,15},{8,0},{9,1},... | collective-permute-start | bytes 73736 | tf_op jit(solution)/shard_map/ppermute | solution.py:272
  16.3 5.6 %collective-permute-start.3 = (bf16[48,512]{1,0:T(8,128)(2,1)S(1)}, bf16[48,512]{1,0:T(8,128)(2,1)S(1)}, u32[]{:S(2)}, u32[]{:S(2)}) collective-permute-start(bf16[48,512]{1,0:T(8,128)(2,1)S(1)} %pad_maximum_fusion.2), channel_id=1, source_target_pairs={{0,6},{1,7},{2,4},{3,5},{4,2},{5,3},{6,0},{7,1},{8,14},{9,15},{10,... | collective-permute-start | bytes 147464 | tf_op jit(solution)/shard_map/ppermute | solution.py:272
  19.1 4.1 %collective-permute-start.2 = (bf16[48,512]{1,0:T(8,128)(2,1)S(1)}, bf16[48,512]{1,0:T(8,128)(2,1)S(1)}, u32[]{:S(2)}, u32[]{:S(2)}) collective-permute-start(bf16[48,512]{1,0:T(8,128)(2,1)S(1)} %pad_maximum_fusion.2), channel_id=1, source_target_pairs={{0,4},{1,5},{2,6},{3,7},{4,0},{5,1},{6,2},{7,3},{8,12},{9,13},{10,... | collective-permute-start | bytes 147464 | tf_op jit(solution)/shard_map/ppermute | solution.py:272
  19.7 4.1 %collective-permute-start.1 = (bf16[48,512]{1,0:T(8,128)(2,1)S(1)}, bf16[48,512]{1,0:T(8,128)(2,1)S(1)}, u32[]{:S(2)}, u32[]{:S(2)}) collective-permute-start(bf16[48,512]{1,0:T(8,128)(2,1)S(1)} %pad_maximum_fusion.2), channel_id=1, source_target_pairs={{0,2},{1,3},{2,0},{3,1},{4,6},{5,7},{6,4},{7,5},{8,10},{9,11},{10,... | collective-permute-start | bytes 147464 | tf_op jit(solution)/shard_map/ppermute | solution.py:272
  23.8 1.5 %collective-permute-start.4 = (bf16[192,512]{1,0:T(8,128)(2,1)S(1)}, bf16[192,512]{1,0:T(8,128)(2,1)S(1)}, u32[]{:S(2)}, u32[]{:S(2)}) collective-permute-start(bf16[192,512]{1,0:T(8,128)(2,1)S(1)} %pad_maximum_fusion.1), channel_id=1, source_target_pairs={{0,1},{1,0},{2,3},{3,2},{4,5},{5,4},{6,7},{7,6},{8,9},{9,8},{10,11... | collective-permute-start | bytes 589832 | tf_op jit(solution)/shard_map/ppermute | solution.py:272

commit v4 on v3

--- a/solution.py
+++ b/solution.py
@@ -11,7 +11,8 @@
 GELU_A = 0.7978845608028654
 GELU_B = 0.044715
 LANES = 128
-CHUNK = 256
+CHUNK = 512
+TILE = 256
 HASH_STEP = 374761393
 HASH_SEED = -1640531535
 HASH_MIX = 668265263
@@ -71,6 +72,7 @@
     for copy in small[1:3]:
         copy.start()
     fetch(1)
+    small[3].start()
     for f in range(frames):
         lhs[f * block + dense : (f + 1) * block, :] = jnp.zeros((block - dense, chans), jnp.bfloat16)
     row = lax.broadcasted_iota(jnp.int32, (dense * frames, LANES), 0)
@@ -112,6 +114,19 @@
             v = pre[f * block : (f + 1) * block, columns]
             gelu = v * (0.5 + 0.5 * jnp.tanh(GELU_A * v * (1.0 + GELU_B * (v * v))))
             active[:, columns] = gelu if f == 0 else active[:, columns] + gelu
+
+        return run
+
+    def project(columns):
+        def run():
+            sums = []
+            for i in range(clip_dev):
+                low, high = i * pix // 8 * 8, min(-(-(i + 1) * pix // 8) * 8, block)
+                row = lax.broadcasted_iota(jnp.int32, (high - low, 1), 0) + low
+                inside = (row >= i * pix) & (row < (i + 1) * pix)
+                sums.append(jnp.sum(jnp.where(inside, active[low:high, columns], 0.0), axis=0, keepdims=True))
+            pooled = (jnp.concatenate(sums + sums, 0) * (1.0 / (frames * pix))).astype(jnp.bfloat16)
+            return jnp.dot(pooled, proj[columns, :], preferred_element_type=jnp.float32)
 
         return run
 
@@ -132,18 +147,18 @@
     cap = captions[...].astype(jnp.float32)
     cap = cap / jnp.sqrt(jnp.sum(cap * cap, axis=1, keepdims=True) + 1e-06)
     joined[0:caps_dev, :] = cap
-    late = []
+    late, parts = [], []
     for k in range(chunks):
         weight_copies[k].wait()
         if k + 2 < chunks:
             fetch(k + 2)
-        elif k + 2 == chunks:
-            small[3].start()
         pieces = prepare(k + 1) if k + 1 < chunks else []
+        if k + 1 == chunks:
+            small[3].wait()
         part = slice(k * CHUNK, (k + 1) * CHUNK)
-        products = [(f, n) for n in range(chunks) for f in range(frames)]
+        products = [(f, n) for n in range(chans // TILE) for f in range(frames)]
         for count, (f, n) in enumerate(products):
-            columns = slice(n * CHUNK, (n + 1) * CHUNK)
+            columns = slice(n * TILE, (n + 1) * TILE)
             taps = [t for t in range(3) if 0 <= f + t - 1 < frames]
             left = jnp.concatenate([lhs[(f + t - 1) * block : (f + t) * block, part] for t in taps], 1)
             right = jnp.concatenate([weight[t, part, columns] for t in taps], 0)
@@ -155,20 +170,14 @@
             for piece in pieces[done:todo]:
                 piece()
             if k + 1 == chunks:
+                if late:
+                    late.pop(0)()
                 late.append(activate(f, columns))
-                if len(late) > 1:
-                    late.pop(0)()
-    for piece in late:
-        piece()
-    sums = []
-    for i in range(clip_dev):
-        low, high = i * pix // 8 * 8, min(-(-(i + 1) * pix // 8) * 8, block)
-        row = lax.broadcasted_iota(jnp.int32, (high - low, 1), 0) + low
-        inside = (row >= i * pix) & (row < (i + 1) * pix)
-        sums.append(jnp.sum(jnp.where(inside, active[low:high, :], 0.0), axis=0, keepdims=True))
-    pooled = (jnp.concatenate(sums + sums, 0) * (1.0 / (frames * pix))).astype(jnp.bfloat16)
-    small[3].wait()
-    video = jnp.dot(pooled, proj[...], preferred_element_type=jnp.float32)
+                if f == 1 and n:
+                    parts.append(project(slice((n - 1) * TILE, n * TILE))())
+    late.pop(0)()
+    parts.append(project(slice(chans - TILE, chans))())
+    video = functools.reduce(lambda a, b: a + b, parts)
     vnorm = jnp.sqrt(jnp.sum(video * video, axis=1, keepdims=True) + 1e-06)
     vunit = video / vnorm
     unit[0:8, :] = vunit
@@ -256,13 +265,18 @@
         mean = jnp.sum(jnp.where(clip == i, squares, 0.0), axis=0, keepdims=True) * (1.0 / (real * chans))
         scale = jnp.where(clip == i, lax.rsqrt(mean + 1e-06), scale)
     scale = jnp.broadcast_to(scale, (block, LANES))[0:dense]
-    copies = []
     for j in range(tiles):
         lanes = slice(j * LANES, (j + 1) * LANES)
         for f in range(frames):
             natural[j, pl.ds(f, dense, stride=frames), :] = acc[f * block : f * block + dense, lanes] * scale
-        out[j] = (natural[j] + delta[j]).astype(jnp.bfloat16).reshape(dense, frames, LANES)
-        copies.append(pltpu.make_async_copy(out.at[j], out_hbm.at[:, :, lanes], sems.at[j]))
+    copies = []
+    for low in range(0, dense, 56):
+        high = min(low + 56, dense)
+        rows = slice(low * frames, high * frames)
+        for j in range(tiles):
+            value = (natural[j, rows, :] + delta[j, rows, :]).astype(jnp.bfloat16)
+            out[low:high, :, j * LANES : (j + 1) * LANES] = value.reshape(high - low, frames, LANES)
+        copies.append(pltpu.make_async_copy(out.at[low:high], out_hbm.at[low:high], sems.at[low // 56]))
         copies[-1].start()
     for copy in copies:
         copy.wait()
@@ -350,21 +364,21 @@
     for i, steps in enumerate(rounds):
         every = swap(every, blocks, steps)
         if i == 0:
+            every, delta = lax.optimization_barrier((every, delta))
+        if i == 1:
             every, slope = lax.optimization_barrier((every, slope))
-        if i == 1:
-            every, delta = lax.optimization_barrier((every, delta))
     out, loss = pl.pallas_call(
         functools.partial(backward_kernel, (clip_dev, frames, pix, chans, block, caps_dev)),
         out_shape=(shape((dense, frames, chans), bf16), shape((1, clip_dev), f32)),
         in_specs=[vmem] * 7,
         out_specs=(hbm, vmem),
         scratch_shapes=[
-            pltpu.VMEM((tiles, dense, frames, LANES), bf16),
+            pltpu.VMEM((dense, frames, chans), bf16),
             pltpu.VMEM((total, chans), bf16),
             pltpu.VMEM((total, chans), f32),
             pltpu.VMEM((tiles, dense * frames, LANES), f32),
             pltpu.VMEM((1, blocks * group), f32),
-            pltpu.SemaphoreType.DMA((tiles,)),
+            pltpu.SemaphoreType.DMA((-(-dense // 56),)),
         ],
         compiler_params=pltpu.CompilerParams(vmem_limit_bytes=24 << 20),
         name="backward",

time: 34.4 us -> 33.9 us (0.985)
  Pallas kernels: 21.3 us -> 20.8 us
where the time goes in v4:
time: 33.9 us; the launch traced here: 33.8 us
  Pallas kernels  20.8 us (61%)
  starting transfers between devices  7.66 us (23%)
  waiting for transfers between devices  4.48 us (13%)
  between operations  0.83 us (2%)
    pallas_call x1, Pallas kernels, shards(): pl.pallas_call(functools.partial(forward_kernel, (clip_dev, frames, pix,...  9.49 us
    pallas_call x1, Pallas kernels, shards(): pl.pallas_call(functools.partial(backward_kernel, (clip_dev, frames, pix,...  8.48 us
    ppermute x5, starting transfers between devices, swap(): lax.ppermute(held, 'dp', [(i, i ^ step) for i in range(blocks)])  7.66 us
    ppermute x5, waiting for transfers between devices, swap(): lax.ppermute(held, 'dp', [(i, i ^ step) for i in range(blocks)])  4.48 us
    pallas_call x1, Pallas kernels, shards(): pl.pallas_call(slope_kernel, out_shape=shape((total, chans), bf16), in_sp...  1.85 us
    pallas_call x1, Pallas kernels, shards(): pl.pallas_call(delta_kernel, out_shape=shape((tiles, dense * frames, LANE...  0.94 us
  transfers between devices with their start and end apart: 5, of which 4 were waited for; matrix products, arithmetic and copies ran while one was open for 0% of the time, Pallas kernels for 8%

profile of v4, /device:TPU:0, one launch (start us, length us, event | category | flops | bytes accessed | tf_op | source)
XLA Modules:
  0.0 33.8 jit_solution(9930897546420967090)
XLA Ops:
  0.6 9.5 %forward.1 = (bf16[24,512]{1,0:T(8,128)(2,1)S(1)}, f32[16,512]{1,0:T(8,128)S(1)}, f32[800,1024]{1,0:T(8,128)S(1)}, s32[784,128]{1,0:T(8,128)S(1)}, f32[8,128]{1,...) custom-call(s32[4]{0:T(128)} %seeds_hbm.1, s32[4,5]{1,0:T(4,128)} %rows_hbm.1, ...), custom_call_target="tpu_custom_call" | custom-call | tf_op jit(solution)/shard_map/forward/pallas_call | solution.py:302
  10.1 4.1 %collective-permute-start = (bf16[24,512]{1,0:T(8,128)(2,1)S(1)}, bf16[24,512]{1,0:T(8,128)(2,1)S(1)}, u32[]{:S(2)}, u32[]{:S(2)}) collective-permute-start(bf16[24,512]{1,0:T(8,128)(2,1)S(1)} %get-tuple-element.15), channel_id=1, source_target_pairs={{0,8},{1,9},{2,10},{3,11},{4,12},{5,13},{6,14},{7,15},{8,0},{9,1},... | collective-permute-start | bytes 73736 | tf_op jit(solution)/shard_map/ppermute | solution.py:286
  14.2 0.9 %delta.1 = f32[8,784,128]{2,1,0:T(8,128)S(1)} custom-call(s32[784,128]{1,0:T(8,128)S(1)} %get-tuple-element.16.start), custom_call_target="tpu_custom_call" | custom-call | flops 8028160 | bytes 3211264 | tf_op jit(solution)/shard_map/delta/pallas_call | solution.py:350
  15.2 0.9 %collective-permute-done = bf16[24,512]{1,0:T(8,128)(2,1)S(1)} collective-permute-done((bf16[24,512]{1,0:T(8,128)(2,1)S(1)}, bf16[24,512]{1,0:T(8,128)(2,1)S(1)}, u32[]{:S(2)}, u32[]{:S(2)}) %collective-permute-start) | collective-permute-done | bytes 24608 | tf_op jit(solution)/shard_map/ppermute | solution.py:286
  16.0 2.9 %collective-permute-start.3 = (bf16[48,512]{1,0:T(8,128)(2,1)S(1)}, bf16[48,512]{1,0:T(8,128)(2,1)S(1)}, u32[]{:S(2)}, u32[]{:S(2)}) collective-permute-start(bf16[48,512]{1,0:T(8,128)(2,1)S(1)} %pad_maximum_fusion.2), channel_id=1, source_target_pairs={{0,6},{1,7},{2,4},{3,5},{4,2},{5,3},{6,0},{7,1},{8,14},{9,15},{10,... | collective-permute-start | bytes 147464 | tf_op jit(solution)/shard_map/ppermute | solution.py:286
  18.9 0.6 %collective-permute-start.2 = (bf16[48,512]{1,0:T(8,128)(2,1)S(1)}, bf16[48,512]{1,0:T(8,128)(2,1)S(1)}, u32[]{:S(2)}, u32[]{:S(2)}) collective-permute-start(bf16[48,512]{1,0:T(8,128)(2,1)S(1)} %pad_maximum_fusion.2), channel_id=1, source_target_pairs={{0,4},{1,5},{2,6},{3,7},{4,0},{5,1},{6,2},{7,3},{8,12},{9,13},{10,... | collective-permute-start | bytes 147464 | tf_op jit(solution)/shard_map/ppermute | solution.py:286
  19.5 0.1 collective-permute-start.1
  19.5 1.9 %slope.1 = bf16[800,1024]{1,0:T(8,128)(2,1)S(1)} custom-call(f32[800,1024]{1,0:T(8,128)S(1)} %get-tuple-element.18.pre), custom_call_target="tpu_custom_call" | custom-call | flops 13107200 | bytes 4915200 | tf_op jit(solution)/shard_map/slope/pallas_call | solution.py:341
  21.4 0.0 collective-permute-done.3
  21.4 1.6 %collective-permute-done.2 = bf16[48,512]{1,0:T(8,128)(2,1)S(1)} collective-permute-done((bf16[48,512]{1,0:T(8,128)(2,1)S(1)}, bf16[48,512]{1,0:T(8,128)(2,1)S(1)}, u32[]{:S(2)}, u32[]{:S(2)}) %collective-permute-start.2) | collective-permute-done | bytes 49184 | tf_op jit(solution)/shard_map/ppermute | solution.py:286
  23.0 0.6 %collective-permute-done.1 = bf16[48,512]{1,0:T(8,128)(2,1)S(1)} collective-permute-done((bf16[48,512]{1,0:T(8,128)(2,1)S(1)}, bf16[48,512]{1,0:T(8,128)(2,1)S(1)}, u32[]{:S(2)}, u32[]{:S(2)}) %collective-permute-start.1) | collective-permute-done | bytes 49184 | tf_op jit(solution)/shard_map/ppermute | solution.py:286
  23.6 0.1 collective-permute-start.4
  23.7 1.4 %collective-permute-done.4 = bf16[192,512]{1,0:T(8,128)(2,1)S(1)} collective-permute-done((bf16[192,512]{1,0:T(8,128)(2,1)S(1)}, bf16[192,512]{1,0:T(8,128)(2,1)S(1)}, u32[]{:S(2)}, u32[]{:S(2)}) %collective-permute-start.4) | collective-permute-done | bytes 196640 | tf_op jit(solution)/shard_map/ppermute | solution.py:286
  25.1 8.5 %backward.1 = (bf16[196,4,1024]{2,1,0:T(4,128)(2,1)}, f32[1,4]{1,0:T(1,128)}) custom-call(bf16[384,512]{1,0:T(8,128)(2,1)S(1)} %pad_maximum_fusion.every, f32[16,512]{1,0:T(8,128)S(1)} %get-tuple-element.20.unit, f32[8,128]{1,0:T(8,128)S(1)} %get-tuple-element.21.own, bf16[800,1024]{1,0:T(8,128)(2,1)S(1)} %slope.1, f32[8,784,128]{2,1,0:T(8,128)S(1)} %delta.1, ...), custom_call_target="tpu_custom_call" | custom-call | tf_op jit(solution)/shard_map/backward/pallas_call | solution.py:370
  (3 shorter events, 0.0 us)
Async XLA Ops:
  10.1 5.9 %collective-permute-start = (bf16[24,512]{1,0:T(8,128)(2,1)S(1)}, bf16[24,512]{1,0:T(8,128)(2,1)S(1)}, u32[]{:S(2)}, u32[]{:S(2)}) collective-permute-start(bf16[24,512]{1,0:T(8,128)(2,1)S(1)} %get-tuple-element.15), channel_id=1, source_target_pairs={{0,8},{1,9},{2,10},{3,11},{4,12},{5,13},{6,14},{7,15},{8,0},{9,1},... | collective-permute-start | bytes 73736 | tf_op jit(solution)/shard_map/ppermute | solution.py:286
  16.0 5.3 %collective-permute-start.3 = (bf16[48,512]{1,0:T(8,128)(2,1)S(1)}, bf16[48,512]{1,0:T(8,128)(2,1)S(1)}, u32[]{:S(2)}, u32[]{:S(2)}) collective-permute-start(bf16[48,512]{1,0:T(8,128)(2,1)S(1)} %pad_maximum_fusion.2), channel_id=1, source_target_pairs={{0,6},{1,7},{2,4},{3,5},{4,2},{5,3},{6,0},{7,1},{8,14},{9,15},{10,... | collective-permute-start | bytes 147464 | tf_op jit(solution)/shard_map/ppermute | solution.py:286
  18.9 4.1 %collective-permute-start.2 = (bf16[48,512]{1,0:T(8,128)(2,1)S(1)}, bf16[48,512]{1,0:T(8,128)(2,1)S(1)}, u32[]{:S(2)}, u32[]{:S(2)}) collective-permute-start(bf16[48,512]{1,0:T(8,128)(2,1)S(1)} %pad_maximum_fusion.2), channel_id=1, source_target_pairs={{0,4},{1,5},{2,6},{3,7},{4,0},{5,1},{6,2},{7,3},{8,12},{9,13},{10,... | collective-permute-start | bytes 147464 | tf_op jit(solution)/shard_map/ppermute | solution.py:286
  19.5 4.1 %collective-permute-start.1 = (bf16[48,512]{1,0:T(8,128)(2,1)S(1)}, bf16[48,512]{1,0:T(8,128)(2,1)S(1)}, u32[]{:S(2)}, u32[]{:S(2)}) collective-permute-start(bf16[48,512]{1,0:T(8,128)(2,1)S(1)} %pad_maximum_fusion.2), channel_id=1, source_target_pairs={{0,2},{1,3},{2,0},{3,1},{4,6},{5,7},{6,4},{7,5},{8,10},{9,11},{10,... | collective-permute-start | bytes 147464 | tf_op jit(solution)/shard_map/ppermute | solution.py:286
  23.6 1.5 %collective-permute-start.4 = (bf16[192,512]{1,0:T(8,128)(2,1)S(1)}, bf16[192,512]{1,0:T(8,128)(2,1)S(1)}, u32[]{:S(2)}, u32[]{:S(2)}) collective-permute-start(bf16[192,512]{1,0:T(8,128)(2,1)S(1)} %pad_maximum_fusion.1), channel_id=1, source_target_pairs={{0,1},{1,0},{2,3},{3,2},{4,5},{5,4},{6,7},{7,6},{8,9},{9,8},{10,11... | collective-permute-start | bytes 589832 | tf_op jit(solution)/shard_map/ppermute | solution.py:286

commit v5 on v4

--- a/solution.py
+++ b/solution.py
@@ -35,8 +35,8 @@
 
 def forward_kernel(
     dims, seeds_hbm, rows_hbm, clips_hbm, weight_hbm, proj_hbm, captions_hbm,
-    pack, unit, pre, start, own, weight, proj,
-    seeds, rows, clips, captions, natural, lhs, active, joined, clip_sems, weight_sems, sems,
+    pack, unit, pre, delta, own, weight, proj,
+    start, seeds, rows, clips, captions, natural, lhs, active, joined, clip_sems, weight_sems, sems,
 ):
     clip_dev, frames, pix, chans, block = dims
     dense, tiles = clip_dev * pix, chans // LANES
@@ -84,11 +84,13 @@
     for i in range(clip_dev):
         seed = jnp.where(clip == i, seeds[i], seed)
     start[...] = seed * jnp.int32(HASH_SEED) + first * jnp.int32(HASH_STEP)
+    for j in range(tiles):
+        delta[j] = signs(start[...] + wrap(j * LANES * HASH_STEP))
 
     def hash_piece(j, rows):
         def run():
             x = clips[j, rows.start // frames : rows.stop // frames].reshape(rows.stop - rows.start, LANES)
-            natural[j, rows, :] = x.astype(jnp.float32) + signs(start[rows, :] + wrap(j * LANES * HASH_STEP))
+            natural[j, rows, :] = x.astype(jnp.float32) + delta[j, rows, :]
 
         return run
 
@@ -192,11 +194,6 @@
     t = jnp.tanh(GELU_A * v * (1.0 + GELU_B * square))
     inner = GELU_A * (1.0 + 3.0 * GELU_B * square)
     slope[...] = (0.5 + 0.5 * t + 0.5 * v * (1.0 - t * t) * inner).astype(jnp.bfloat16)
-
-
-def delta_kernel(start, delta):
-    for j in range(delta.shape[0]):
-        delta[j] = signs(start[...] + wrap(j * LANES * HASH_STEP))
 
 
 def backward_kernel(
@@ -299,13 +296,13 @@
     shape = jax.ShapeDtypeStruct
     vmem = pl.BlockSpec(memory_space=pltpu.VMEM)
     hbm = pl.BlockSpec(memory_space=pltpu.HBM)
-    pack, unit, pre, start, own, weight, proj = pl.pallas_call(
+    pack, unit, pre, delta, own, weight, proj = pl.pallas_call(
         functools.partial(forward_kernel, (clip_dev, frames, pix, chans, block)),
         out_shape=(
             shape((group, embed), bf16),
             shape((16, embed), f32),
             shape((total, chans), f32),
-            shape((dense * frames, LANES), i32),
+            shape((tiles, dense * frames, LANES), f32),
             shape((8, -(-caps_dev // LANES) * LANES), f32),
             shape((3, chans, chans), bf16),
             shape((chans, embed), bf16),
@@ -313,6 +310,7 @@
         in_specs=[hbm] * 6,
         out_specs=(vmem,) * 7,
         scratch_shapes=[
+            pltpu.VMEM((dense * frames, LANES), i32),
             pltpu.SMEM((clip_dev,), i32),
             pltpu.SMEM(caption_rows.shape, i32),
             pltpu.VMEM((tiles, dense, frames, LANES), bf16),
@@ -347,15 +345,6 @@
         cost_estimate=pl.CostEstimate(flops=16 * total * chans, bytes_accessed=6 * total * chans, transcendentals=total * chans),
         name="slope",
     )(pre)
-    delta = pl.pallas_call(
-        delta_kernel,
-        out_shape=shape((tiles, dense * frames, LANES), f32),
-        in_specs=[vmem],
-        out_specs=vmem,
-        compiler_params=pltpu.CompilerParams(vmem_limit_bytes=8 << 20),
-        cost_estimate=pl.CostEstimate(flops=10 * dense * frames * chans, bytes_accessed=4 * dense * frames * chans, transcendentals=0),
-        name="delta",
-    )(start)
     if blocks == 16:
         rounds = [(8,), (2, 4, 6), (1,)]
     else:
@@ -364,8 +353,6 @@
     for i, steps in enumerate(rounds):
         every = swap(every, blocks, steps)
         if i == 0:
-            every, delta = lax.optimization_barrier((every, delta))
-        if i == 1:
             every, slope = lax.optimization_barrier((every, slope))
     out, loss = pl.pallas_call(
         functools.partial(backward_kernel, (clip_dev, frames, pix, chans, block, caps_dev)),

time: 33.9 us -> 33.5 us (0.988)
  Pallas kernels: 20.8 us -> 19.4 us
  waiting for transfers between devices: 4.48 us -> 5.31 us
    pallas_call x1 -> x0, Pallas kernels: 0.94 us -> none  [shards(): pl.pallas_call(delta_kernel, out_shape=shape((tiles, dense * frames, LANE...]
    ppermute x5, waiting for transfers between devices: 4.48 us -> 5.31 us  [swap(): lax.ppermute(held, 'dp', [(i, i ^ step) for i in range(blocks)])]
    pallas_call x1, Pallas kernels: 9.49 us -> 9.09 us  [shards(): pl.pallas_call(functools.partial(forward_kernel, (clip_dev, frames, pix,...]
  transfers between devices with their start and end apart: 5 -> 5, of which waited for: 4 -> 4; matrix products, arithmetic and copies ran while one was open for 0% -> 0% of each run, Pallas kernels for 8% -> 6%
where the time goes in v5:
time: 33.5 us; the launch traced here: 33.4 us
  Pallas kernels  19.4 us (58%)
  starting transfers between devices  7.73 us (23%)
  waiting for transfers between devices  5.31 us (16%)
  between operations  0.86 us (3%)
    pallas_call x1, Pallas kernels, shards(): pl.pallas_call(functools.partial(forward_kernel, (clip_dev, frames, pix,...  9.09 us
    pallas_call x1, Pallas kernels, shards(): pl.pallas_call(functools.partial(backward_kernel, (clip_dev, frames, pix,...  8.47 us
    ppermute x5, starting transfers between devices, swap(): lax.ppermute(held, 'dp', [(i, i ^ step) for i in range(blocks)])  7.73 us
    ppermute x5, waiting for transfers between devices, swap(): lax.ppermute(held, 'dp', [(i, i ^ step) for i in range(blocks)])  5.31 us
    pallas_call x1, Pallas kernels, shards(): pl.pallas_call(slope_kernel, out_shape=shape((total, chans), bf16), in_sp...  1.85 us
  transfers between devices with their start and end apart: 5, of which 4 were waited for; matrix products, arithmetic and copies ran while one was open for 0% of the time, Pallas kernels for 6%

profile of v5, /device:TPU:0, one launch (start us, length us, event | category | flops | bytes accessed | tf_op | source)
XLA Modules:
  0.0 33.4 jit_solution(10679086549050909322)
XLA Ops:
  0.6 9.1 %forward.1 = (bf16[24,512]{1,0:T(8,128)(2,1)S(1)}, f32[16,512]{1,0:T(8,128)S(1)}, f32[800,1024]{1,0:T(8,128)S(1)}, f32[8,784,128]{2,1,0:T(8,128)S(1)}, f32[8,128...) custom-call(s32[4]{0:T(128)} %seeds_hbm.1, s32[4,5]{1,0:T(4,128)} %rows_hbm.1, ...), custom_call_target="tpu_custom_call" | custom-call | tf_op jit(solution)/shard_map/forward/pallas_call | solution.py:299
  9.7 4.1 %collective-permute-start = (bf16[24,512]{1,0:T(8,128)(2,1)S(1)}, bf16[24,512]{1,0:T(8,128)(2,1)S(1)}, u32[]{:S(2)}, u32[]{:S(2)}) collective-permute-start(bf16[24,512]{1,0:T(8,128)(2,1)S(1)} %get-tuple-element.13), channel_id=1, source_target_pairs={{0,8},{1,9},{2,10},{3,11},{4,12},{5,13},{6,14},{7,15},{8,0},{9,1},... | collective-permute-start | bytes 73736 | tf_op jit(solution)/shard_map/ppermute | solution.py:283
  13.8 1.9 %slope.1 = bf16[800,1024]{1,0:T(8,128)(2,1)S(1)} custom-call(f32[800,1024]{1,0:T(8,128)S(1)} %get-tuple-element.14.pre), custom_call_target="tpu_custom_call" | custom-call | flops 13107200 | bytes 4915200 | tf_op jit(solution)/shard_map/slope/pallas_call | solution.py:339
  15.7 0.0 collective-permute-done
  15.7 2.8 %collective-permute-start.3 = (bf16[48,512]{1,0:T(8,128)(2,1)S(1)}, bf16[48,512]{1,0:T(8,128)(2,1)S(1)}, u32[]{:S(2)}, u32[]{:S(2)}) collective-permute-start(bf16[48,512]{1,0:T(8,128)(2,1)S(1)} %pad_maximum_fusion.1), channel_id=1, source_target_pairs={{0,6},{1,7},{2,4},{3,5},{4,2},{5,3},{6,0},{7,1},{8,14},{9,15},{10,... | collective-permute-start | bytes 147464 | tf_op jit(solution)/shard_map/ppermute | solution.py:283
  18.5 0.6 %collective-permute-start.2 = (bf16[48,512]{1,0:T(8,128)(2,1)S(1)}, bf16[48,512]{1,0:T(8,128)(2,1)S(1)}, u32[]{:S(2)}, u32[]{:S(2)}) collective-permute-start(bf16[48,512]{1,0:T(8,128)(2,1)S(1)} %pad_maximum_fusion.1), channel_id=1, source_target_pairs={{0,4},{1,5},{2,6},{3,7},{4,0},{5,1},{6,2},{7,3},{8,12},{9,13},{10,... | collective-permute-start | bytes 147464 | tf_op jit(solution)/shard_map/ppermute | solution.py:283
  19.1 0.2 collective-permute-start.1
  19.3 2.0 %collective-permute-done.3 = bf16[48,512]{1,0:T(8,128)(2,1)S(1)} collective-permute-done((bf16[48,512]{1,0:T(8,128)(2,1)S(1)}, bf16[48,512]{1,0:T(8,128)(2,1)S(1)}, u32[]{:S(2)}, u32[]{:S(2)}) %collective-permute-start.3) | collective-permute-done | bytes 49184 | tf_op jit(solution)/shard_map/ppermute | solution.py:283
  21.3 1.3 %collective-permute-done.2 = bf16[48,512]{1,0:T(8,128)(2,1)S(1)} collective-permute-done((bf16[48,512]{1,0:T(8,128)(2,1)S(1)}, bf16[48,512]{1,0:T(8,128)(2,1)S(1)}, u32[]{:S(2)}, u32[]{:S(2)}) %collective-permute-start.2) | collective-permute-done | bytes 49184 | tf_op jit(solution)/shard_map/ppermute | solution.py:283
  22.6 0.6 %collective-permute-done.1 = bf16[48,512]{1,0:T(8,128)(2,1)S(1)} collective-permute-done((bf16[48,512]{1,0:T(8,128)(2,1)S(1)}, bf16[48,512]{1,0:T(8,128)(2,1)S(1)}, u32[]{:S(2)}, u32[]{:S(2)}) %collective-permute-start.1) | collective-permute-done | bytes 49184 | tf_op jit(solution)/shard_map/ppermute | solution.py:283
  23.2 0.1 collective-permute-start.4
  23.3 1.4 %collective-permute-done.4 = bf16[192,512]{1,0:T(8,128)(2,1)S(1)} collective-permute-done((bf16[192,512]{1,0:T(8,128)(2,1)S(1)}, bf16[192,512]{1,0:T(8,128)(2,1)S(1)}, u32[]{:S(2)}, u32[]{:S(2)}) %collective-permute-start.4) | collective-permute-done | bytes 196640 | tf_op jit(solution)/shard_map/ppermute | solution.py:283
  24.7 8.5 %backward.1 = (bf16[196,4,1024]{2,1,0:T(4,128)(2,1)}, f32[1,4]{1,0:T(1,128)}) custom-call(bf16[384,512]{1,0:T(8,128)(2,1)S(1)} %constant_dynamic-update-slice_fusion.every, f32[16,512]{1,0:T(8,128)S(1)} %get-tuple-element.16.unit, f32[8,128]{1,0:T(8,128)S(1)} %get-tuple-element.17.own, bf16[800,1024]{1,0:T(8,128)(2,1)S(1)} %slope.1, ...), custom_call_target="tpu_custom_call" | custom-call | tf_op jit(solution)/shard_map/backward/pallas_call | solution.py:357
  (7 shorter events, 0.1 us)
Async XLA Ops:
  9.7 6.0 %collective-permute-start = (bf16[24,512]{1,0:T(8,128)(2,1)S(1)}, bf16[24,512]{1,0:T(8,128)(2,1)S(1)}, u32[]{:S(2)}, u32[]{:S(2)}) collective-permute-start(bf16[24,512]{1,0:T(8,128)(2,1)S(1)} %get-tuple-element.13), channel_id=1, source_target_pairs={{0,8},{1,9},{2,10},{3,11},{4,12},{5,13},{6,14},{7,15},{8,0},{9,1},... | collective-permute-start | bytes 73736 | tf_op jit(solution)/shard_map/ppermute | solution.py:283
  15.7 5.6 %collective-permute-start.3 = (bf16[48,512]{1,0:T(8,128)(2,1)S(1)}, bf16[48,512]{1,0:T(8,128)(2,1)S(1)}, u32[]{:S(2)}, u32[]{:S(2)}) collective-permute-start(bf16[48,512]{1,0:T(8,128)(2,1)S(1)} %pad_maximum_fusion.1), channel_id=1, source_target_pairs={{0,6},{1,7},{2,4},{3,5},{4,2},{5,3},{6,0},{7,1},{8,14},{9,15},{10,... | collective-permute-start | bytes 147464 | tf_op jit(solution)/shard_map/ppermute | solution.py:283
  18.5 4.1 %collective-permute-start.2 = (bf16[48,512]{1,0:T(8,128)(2,1)S(1)}, bf16[48,512]{1,0:T(8,128)(2,1)S(1)}, u32[]{:S(2)}, u32[]{:S(2)}) collective-permute-start(bf16[48,512]{1,0:T(8,128)(2,1)S(1)} %pad_maximum_fusion.1), channel_id=1, source_target_pairs={{0,4},{1,5},{2,6},{3,7},{4,0},{5,1},{6,2},{7,3},{8,12},{9,13},{10,... | collective-permute-start | bytes 147464 | tf_op jit(solution)/shard_map/ppermute | solution.py:283
  19.1 4.1 %collective-permute-start.1 = (bf16[48,512]{1,0:T(8,128)(2,1)S(1)}, bf16[48,512]{1,0:T(8,128)(2,1)S(1)}, u32[]{:S(2)}, u32[]{:S(2)}) collective-permute-start(bf16[48,512]{1,0:T(8,128)(2,1)S(1)} %pad_maximum_fusion.1), channel_id=1, source_target_pairs={{0,2},{1,3},{2,0},{3,1},{4,6},{5,7},{6,4},{7,5},{8,10},{9,11},{10,... | collective-permute-start | bytes 147464 | tf_op jit(solution)/shard_map/ppermute | solution.py:283
  23.2 1.5 %collective-permute-start.4 = (bf16[192,512]{1,0:T(8,128)(2,1)S(1)}, bf16[192,512]{1,0:T(8,128)(2,1)S(1)}, u32[]{:S(2)}, u32[]{:S(2)}) collective-permute-start(bf16[192,512]{1,0:T(8,128)(2,1)S(1)} %pad_maximum_fusion), channel_id=1, source_target_pairs={{0,1},{1,0},{2,3},{3,2},{4,5},{5,4},{6,7},{7,6},{8,9},{9,8},{10,11... | collective-permute-start | bytes 589832 | tf_op jit(solution)/shard_map/ppermute | solution.py:283

commit v6 on v5

--- a/solution.py
+++ b/solution.py
@@ -12,7 +12,7 @@
 GELU_B = 0.044715
 LANES = 128
 CHUNK = 512
-TILE = 256
+TILE = 512
 HASH_STEP = 374761393
 HASH_SEED = -1640531535
 HASH_MIX = 668265263

time: 33.5 us -> 33.3 us (level)
  no operation moved by 1% of the time
where the time goes in v6:
time: 33.3 us; the launch traced here: 33.1 us
  Pallas kernels  19.2 us (58%)
  starting transfers between devices  7.7 us (23%)
  waiting for transfers between devices  5.31 us (16%)
  between operations  0.86 us (3%)
    pallas_call x1, Pallas kernels, shards(): pl.pallas_call(functools.partial(forward_kernel, (clip_dev, frames, pix,...  8.91 us
    pallas_call x1, Pallas kernels, shards(): pl.pallas_call(functools.partial(backward_kernel, (clip_dev, frames, pix,...  8.45 us
    ppermute x5, starting transfers between devices, swap(): lax.ppermute(held, 'dp', [(i, i ^ step) for i in range(blocks)])  7.7 us
    ppermute x5, waiting for transfers between devices, swap(): lax.ppermute(held, 'dp', [(i, i ^ step) for i in range(blocks)])  5.31 us
    pallas_call x1, Pallas kernels, shards(): pl.pallas_call(slope_kernel, out_shape=shape((total, chans), bf16), in_sp...  1.85 us
  transfers between devices with their start and end apart: 5, of which 4 were waited for; matrix products, arithmetic and copies ran while one was open for 0% of the time, Pallas kernels for 6%

profile of v6, /device:TPU:0, one launch (start us, length us, event | category | flops | bytes accessed | tf_op | source)
XLA Modules:
  0.0 33.1 jit_solution(10263519171271183696)
XLA Ops:
  0.6 8.9 %forward.1 = (bf16[24,512]{1,0:T(8,128)(2,1)S(1)}, f32[16,512]{1,0:T(8,128)S(1)}, f32[800,1024]{1,0:T(8,128)S(1)}, f32[8,784,128]{2,1,0:T(8,128)S(1)}, f32[8,128...) custom-call(s32[4]{0:T(128)} %seeds_hbm.1, s32[4,5]{1,0:T(4,128)} %rows_hbm.1, ...), custom_call_target="tpu_custom_call" | custom-call | tf_op jit(solution)/shard_map/forward/pallas_call | solution.py:299
  9.5 4.1 %collective-permute-start = (bf16[24,512]{1,0:T(8,128)(2,1)S(1)}, bf16[24,512]{1,0:T(8,128)(2,1)S(1)}, u32[]{:S(2)}, u32[]{:S(2)}) collective-permute-start(bf16[24,512]{1,0:T(8,128)(2,1)S(1)} %get-tuple-element.13), channel_id=1, source_target_pairs={{0,8},{1,9},{2,10},{3,11},{4,12},{5,13},{6,14},{7,15},{8,0},{9,1},... | collective-permute-start | bytes 73736 | tf_op jit(solution)/shard_map/ppermute | solution.py:283
  13.6 1.9 %slope.1 = bf16[800,1024]{1,0:T(8,128)(2,1)S(1)} custom-call(f32[800,1024]{1,0:T(8,128)S(1)} %get-tuple-element.14.pre), custom_call_target="tpu_custom_call" | custom-call | flops 13107200 | bytes 4915200 | tf_op jit(solution)/shard_map/slope/pallas_call | solution.py:339
  15.5 0.0 collective-permute-done
  15.5 2.8 %collective-permute-start.3 = (bf16[48,512]{1,0:T(8,128)(2,1)S(1)}, bf16[48,512]{1,0:T(8,128)(2,1)S(1)}, u32[]{:S(2)}, u32[]{:S(2)}) collective-permute-start(bf16[48,512]{1,0:T(8,128)(2,1)S(1)} %pad_maximum_fusion.1), channel_id=1, source_target_pairs={{0,6},{1,7},{2,4},{3,5},{4,2},{5,3},{6,0},{7,1},{8,14},{9,15},{10,... | collective-permute-start | bytes 147464 | tf_op jit(solution)/shard_map/ppermute | solution.py:283
  18.3 0.6 %collective-permute-start.2 = (bf16[48,512]{1,0:T(8,128)(2,1)S(1)}, bf16[48,512]{1,0:T(8,128)(2,1)S(1)}, u32[]{:S(2)}, u32[]{:S(2)}) collective-permute-start(bf16[48,512]{1,0:T(8,128)(2,1)S(1)} %pad_maximum_fusion.1), channel_id=1, source_target_pairs={{0,4},{1,5},{2,6},{3,7},{4,0},{5,1},{6,2},{7,3},{8,12},{9,13},{10,... | collective-permute-start | bytes 147464 | tf_op jit(solution)/shard_map/ppermute | solution.py:283
  18.9 0.2 collective-permute-start.1
  19.1 2.0 %collective-permute-done.3 = bf16[48,512]{1,0:T(8,128)(2,1)S(1)} collective-permute-done((bf16[48,512]{1,0:T(8,128)(2,1)S(1)}, bf16[48,512]{1,0:T(8,128)(2,1)S(1)}, u32[]{:S(2)}, u32[]{:S(2)}) %collective-permute-start.3) | collective-permute-done | bytes 49184 | tf_op jit(solution)/shard_map/ppermute | solution.py:283
  21.1 1.3 %collective-permute-done.2 = bf16[48,512]{1,0:T(8,128)(2,1)S(1)} collective-permute-done((bf16[48,512]{1,0:T(8,128)(2,1)S(1)}, bf16[48,512]{1,0:T(8,128)(2,1)S(1)}, u32[]{:S(2)}, u32[]{:S(2)}) %collective-permute-start.2) | collective-permute-done | bytes 49184 | tf_op jit(solution)/shard_map/ppermute | solution.py:283
  22.4 0.6 %collective-permute-done.1 = bf16[48,512]{1,0:T(8,128)(2,1)S(1)} collective-permute-done((bf16[48,512]{1,0:T(8,128)(2,1)S(1)}, bf16[48,512]{1,0:T(8,128)(2,1)S(1)}, u32[]{:S(2)}, u32[]{:S(2)}) %collective-permute-start.1) | collective-permute-done | bytes 49184 | tf_op jit(solution)/shard_map/ppermute | solution.py:283
  23.0 0.1 collective-permute-start.4
  23.1 1.4 %collective-permute-done.4 = bf16[192,512]{1,0:T(8,128)(2,1)S(1)} collective-permute-done((bf16[192,512]{1,0:T(8,128)(2,1)S(1)}, bf16[192,512]{1,0:T(8,128)(2,1)S(1)}, u32[]{:S(2)}, u32[]{:S(2)}) %collective-permute-start.4) | collective-permute-done | bytes 196640 | tf_op jit(solution)/shard_map/ppermute | solution.py:283
  24.5 8.5 %backward.1 = (bf16[196,4,1024]{2,1,0:T(4,128)(2,1)}, f32[1,4]{1,0:T(1,128)}) custom-call(bf16[384,512]{1,0:T(8,128)(2,1)S(1)} %constant_dynamic-update-slice_fusion.every, f32[16,512]{1,0:T(8,128)S(1)} %get-tuple-element.16.unit, f32[8,128]{1,0:T(8,128)S(1)} %get-tuple-element.17.own, bf16[800,1024]{1,0:T(8,128)(2,1)S(1)} %slope.1, ...), custom_call_target="tpu_custom_call" | custom-call | tf_op jit(solution)/shard_map/backward/pallas_call | solution.py:357
  (7 shorter events, 0.1 us)
Async XLA Ops:
  9.5 5.9 %collective-permute-start = (bf16[24,512]{1,0:T(8,128)(2,1)S(1)}, bf16[24,512]{1,0:T(8,128)(2,1)S(1)}, u32[]{:S(2)}, u32[]{:S(2)}) collective-permute-start(bf16[24,512]{1,0:T(8,128)(2,1)S(1)} %get-tuple-element.13), channel_id=1, source_target_pairs={{0,8},{1,9},{2,10},{3,11},{4,12},{5,13},{6,14},{7,15},{8,0},{9,1},... | collective-permute-start | bytes 73736 | tf_op jit(solution)/shard_map/ppermute | solution.py:283
  15.5 5.6 %collective-permute-start.3 = (bf16[48,512]{1,0:T(8,128)(2,1)S(1)}, bf16[48,512]{1,0:T(8,128)(2,1)S(1)}, u32[]{:S(2)}, u32[]{:S(2)}) collective-permute-start(bf16[48,512]{1,0:T(8,128)(2,1)S(1)} %pad_maximum_fusion.1), channel_id=1, source_target_pairs={{0,6},{1,7},{2,4},{3,5},{4,2},{5,3},{6,0},{7,1},{8,14},{9,15},{10,... | collective-permute-start | bytes 147464 | tf_op jit(solution)/shard_map/ppermute | solution.py:283
  18.3 4.1 %collective-permute-start.2 = (bf16[48,512]{1,0:T(8,128)(2,1)S(1)}, bf16[48,512]{1,0:T(8,128)(2,1)S(1)}, u32[]{:S(2)}, u32[]{:S(2)}) collective-permute-start(bf16[48,512]{1,0:T(8,128)(2,1)S(1)} %pad_maximum_fusion.1), channel_id=1, source_target_pairs={{0,4},{1,5},{2,6},{3,7},{4,0},{5,1},{6,2},{7,3},{8,12},{9,13},{10,... | collective-permute-start | bytes 147464 | tf_op jit(solution)/shard_map/ppermute | solution.py:283
  18.9 4.1 %collective-permute-start.1 = (bf16[48,512]{1,0:T(8,128)(2,1)S(1)}, bf16[48,512]{1,0:T(8,128)(2,1)S(1)}, u32[]{:S(2)}, u32[]{:S(2)}) collective-permute-start(bf16[48,512]{1,0:T(8,128)(2,1)S(1)} %pad_maximum_fusion.1), channel_id=1, source_target_pairs={{0,2},{1,3},{2,0},{3,1},{4,6},{5,7},{6,4},{7,5},{8,10},{9,11},{10,... | collective-permute-start | bytes 147464 | tf_op jit(solution)/shard_map/ppermute | solution.py:283
  23.0 1.5 %collective-permute-start.4 = (bf16[192,512]{1,0:T(8,128)(2,1)S(1)}, bf16[192,512]{1,0:T(8,128)(2,1)S(1)}, u32[]{:S(2)}, u32[]{:S(2)}) collective-permute-start(bf16[192,512]{1,0:T(8,128)(2,1)S(1)} %pad_maximum_fusion), channel_id=1, source_target_pairs={{0,1},{1,0},{2,3},{3,2},{4,5},{5,4},{6,7},{7,6},{8,9},{9,8},{10,11... | collective-permute-start | bytes 589832 | tf_op jit(solution)/shard_map/ppermute | solution.py:283

commit v7 on v6

--- a/solution.py
+++ b/solution.py
@@ -249,8 +249,8 @@
         lhs[rows, :] = (slope[rows, :].astype(jnp.float32) * spread).astype(jnp.bfloat16)
     rest = (frames - 1) * block
     turned = (((1,), (1,)), ((), ()))
-    acc[...] = lax.dot_general(lhs[...], weight[1], turned, preferred_element_type=jnp.float32)
-    acc[0:rest, :] += lax.dot_general(lhs[block:, :], weight[0], turned, preferred_element_type=jnp.float32)
+    acc[...] = lax.dot_general(lhs[0 : rest + block, :], weight[1], turned, preferred_element_type=jnp.float32)
+    acc[0:rest, :] += lax.dot_general(lhs[block : rest + block, :], weight[0], turned, preferred_element_type=jnp.float32)
     acc[block:, :] += lax.dot_general(lhs[0:rest, :], weight[2], turned, preferred_element_type=jnp.float32)
     squares = jnp.zeros((block, chans), jnp.float32)
     for f in range(frames):
@@ -315,8 +315,8 @@
             pltpu.SMEM(caption_rows.shape, i32),
             pltpu.VMEM((tiles, dense, frames, LANES), bf16),
             pltpu.VMEM((caps_dev, embed), bf16),
-            pltpu.VMEM((tiles, dense * frames, LANES), f32),
-            pltpu.VMEM((total, chans), bf16),
+            pltpu.VMEM((tiles, total, LANES), f32),
+            pltpu.VMEM((total + 16, chans), bf16),
             pltpu.VMEM((block, chans), f32),
             pltpu.VMEM((group, embed), f32),
             pltpu.SemaphoreType.DMA((tiles,)),
@@ -361,9 +361,9 @@
         out_specs=(hbm, vmem),
         scratch_shapes=[
             pltpu.VMEM((dense, frames, chans), bf16),
-            pltpu.VMEM((total, chans), bf16),
+            pltpu.VMEM((total + 16, chans), bf16),
             pltpu.VMEM((total, chans), f32),
-            pltpu.VMEM((tiles, dense * frames, LANES), f32),
+            pltpu.VMEM((tiles, total, LANES), f32),
             pltpu.VMEM((1, blocks * group), f32),
             pltpu.SemaphoreType.DMA((-(-dense // 56),)),
         ],

time: 33.3 us -> 33.3 us (level)
  no operation moved by 1% of the time
where the time goes in v7:
time: 33.3 us; the launch traced here: 33.2 us
  Pallas kernels  19.2 us (58%)
  starting transfers between devices  7.73 us (23%)
  waiting for transfers between devices  5.31 us (16%)
  between operations  0.86 us (3%)
    pallas_call x1, Pallas kernels, shards(): pl.pallas_call(functools.partial(forward_kernel, (clip_dev, frames, pix,...  8.9 us
    pallas_call x1, Pallas kernels, shards(): pl.pallas_call(functools.partial(backward_kernel, (clip_dev, frames, pix,...  8.46 us
    ppermute x5, starting transfers between devices, swap(): lax.ppermute(held, 'dp', [(i, i ^ step) for i in range(blocks)])  7.73 us
    ppermute x5, waiting for transfers between devices, swap(): lax.ppermute(held, 'dp', [(i, i ^ step) for i in range(blocks)])  5.31 us
    pallas_call x1, Pallas kernels, shards(): pl.pallas_call(slope_kernel, out_shape=shape((total, chans), bf16), in_sp...  1.85 us
  transfers between devices with their start and end apart: 5, of which 4 were waited for; matrix products, arithmetic and copies ran while one was open for 0% of the time, Pallas kernels for 6%

profile of v7, /device:TPU:0, one launch (start us, length us, event | category | flops | bytes accessed | tf_op | source)
XLA Modules:
  0.0 33.2 jit_solution(11055543330984946288)
XLA Ops:
  0.6 8.9 %forward.1 = (bf16[24,512]{1,0:T(8,128)(2,1)S(1)}, f32[16,512]{1,0:T(8,128)S(1)}, f32[800,1024]{1,0:T(8,128)S(1)}, f32[8,784,128]{2,1,0:T(8,128)S(1)}, f32[8,128...) custom-call(s32[4]{0:T(128)} %seeds_hbm.1, s32[4,5]{1,0:T(4,128)} %rows_hbm.1, ...), custom_call_target="tpu_custom_call" | custom-call | tf_op jit(solution)/shard_map/forward/pallas_call | solution.py:299
  9.5 4.1 %collective-permute-start = (bf16[24,512]{1,0:T(8,128)(2,1)S(1)}, bf16[24,512]{1,0:T(8,128)(2,1)S(1)}, u32[]{:S(2)}, u32[]{:S(2)}) collective-permute-start(bf16[24,512]{1,0:T(8,128)(2,1)S(1)} %get-tuple-element.13), channel_id=1, source_target_pairs={{0,8},{1,9},{2,10},{3,11},{4,12},{5,13},{6,14},{7,15},{8,0},{9,1},... | collective-permute-start | bytes 73736 | tf_op jit(solution)/shard_map/ppermute | solution.py:283
  13.7 1.9 %slope.1 = bf16[800,1024]{1,0:T(8,128)(2,1)S(1)} custom-call(f32[800,1024]{1,0:T(8,128)S(1)} %get-tuple-element.14.pre), custom_call_target="tpu_custom_call" | custom-call | flops 13107200 | bytes 4915200 | tf_op jit(solution)/shard_map/slope/pallas_call | solution.py:339
  15.5 0.0 collective-permute-done
  15.5 2.8 %collective-permute-start.3 = (bf16[48,512]{1,0:T(8,128)(2,1)S(1)}, bf16[48,512]{1,0:T(8,128)(2,1)S(1)}, u32[]{:S(2)}, u32[]{:S(2)}) collective-permute-start(bf16[48,512]{1,0:T(8,128)(2,1)S(1)} %pad_maximum_fusion.1), channel_id=1, source_target_pairs={{0,6},{1,7},{2,4},{3,5},{4,2},{5,3},{6,0},{7,1},{8,14},{9,15},{10,... | collective-permute-start | bytes 147464 | tf_op jit(solution)/shard_map/ppermute | solution.py:283
  18.3 0.6 %collective-permute-start.2 = (bf16[48,512]{1,0:T(8,128)(2,1)S(1)}, bf16[48,512]{1,0:T(8,128)(2,1)S(1)}, u32[]{:S(2)}, u32[]{:S(2)}) collective-permute-start(bf16[48,512]{1,0:T(8,128)(2,1)S(1)} %pad_maximum_fusion.1), channel_id=1, source_target_pairs={{0,4},{1,5},{2,6},{3,7},{4,0},{5,1},{6,2},{7,3},{8,12},{9,13},{10,... | collective-permute-start | bytes 147464 | tf_op jit(solution)/shard_map/ppermute | solution.py:283
  18.9 0.2 collective-permute-start.1
  19.1 2.0 %collective-permute-done.3 = bf16[48,512]{1,0:T(8,128)(2,1)S(1)} collective-permute-done((bf16[48,512]{1,0:T(8,128)(2,1)S(1)}, bf16[48,512]{1,0:T(8,128)(2,1)S(1)}, u32[]{:S(2)}, u32[]{:S(2)}) %collective-permute-start.3) | collective-permute-done | bytes 49184 | tf_op jit(solution)/shard_map/ppermute | solution.py:283
  21.1 1.3 %collective-permute-done.2 = bf16[48,512]{1,0:T(8,128)(2,1)S(1)} collective-permute-done((bf16[48,512]{1,0:T(8,128)(2,1)S(1)}, bf16[48,512]{1,0:T(8,128)(2,1)S(1)}, u32[]{:S(2)}, u32[]{:S(2)}) %collective-permute-start.2) | collective-permute-done | bytes 49184 | tf_op jit(solution)/shard_map/ppermute | solution.py:283
  22.4 0.6 %collective-permute-done.1 = bf16[48,512]{1,0:T(8,128)(2,1)S(1)} collective-permute-done((bf16[48,512]{1,0:T(8,128)(2,1)S(1)}, bf16[48,512]{1,0:T(8,128)(2,1)S(1)}, u32[]{:S(2)}, u32[]{:S(2)}) %collective-permute-start.1) | collective-permute-done | bytes 49184 | tf_op jit(solution)/shard_map/ppermute | solution.py:283
  23.0 0.1 collective-permute-start.4
  23.1 1.4 %collective-permute-done.4 = bf16[192,512]{1,0:T(8,128)(2,1)S(1)} collective-permute-done((bf16[192,512]{1,0:T(8,128)(2,1)S(1)}, bf16[192,512]{1,0:T(8,128)(2,1)S(1)}, u32[]{:S(2)}, u32[]{:S(2)}) %collective-permute-start.4) | collective-permute-done | bytes 196640 | tf_op jit(solution)/shard_map/ppermute | solution.py:283
  24.6 8.5 %backward.1 = (bf16[196,4,1024]{2,1,0:T(4,128)(2,1)}, f32[1,4]{1,0:T(1,128)}) custom-call(bf16[384,512]{1,0:T(8,128)(2,1)S(1)} %constant_dynamic-update-slice_fusion.every, f32[16,512]{1,0:T(8,128)S(1)} %get-tuple-element.16.unit, f32[8,128]{1,0:T(8,128)S(1)} %get-tuple-element.17.own, bf16[800,1024]{1,0:T(8,128)(2,1)S(1)} %slope.1, ...), custom_call_target="tpu_custom_call" | custom-call | tf_op jit(solution)/shard_map/backward/pallas_call | solution.py:357
  (7 shorter events, 0.1 us)
Async XLA Ops:
  9.5 6.0 %collective-permute-start = (bf16[24,512]{1,0:T(8,128)(2,1)S(1)}, bf16[24,512]{1,0:T(8,128)(2,1)S(1)}, u32[]{:S(2)}, u32[]{:S(2)}) collective-permute-start(bf16[24,512]{1,0:T(8,128)(2,1)S(1)} %get-tuple-element.13), channel_id=1, source_target_pairs={{0,8},{1,9},{2,10},{3,11},{4,12},{5,13},{6,14},{7,15},{8,0},{9,1},... | collective-permute-start | bytes 73736 | tf_op jit(solution)/shard_map/ppermute | solution.py:283
  15.5 5.5 %collective-permute-start.3 = (bf16[48,512]{1,0:T(8,128)(2,1)S(1)}, bf16[48,512]{1,0:T(8,128)(2,1)S(1)}, u32[]{:S(2)}, u32[]{:S(2)}) collective-permute-start(bf16[48,512]{1,0:T(8,128)(2,1)S(1)} %pad_maximum_fusion.1), channel_id=1, source_target_pairs={{0,6},{1,7},{2,4},{3,5},{4,2},{5,3},{6,0},{7,1},{8,14},{9,15},{10,... | collective-permute-start | bytes 147464 | tf_op jit(solution)/shard_map/ppermute | solution.py:283
  18.3 4.1 %collective-permute-start.2 = (bf16[48,512]{1,0:T(8,128)(2,1)S(1)}, bf16[48,512]{1,0:T(8,128)(2,1)S(1)}, u32[]{:S(2)}, u32[]{:S(2)}) collective-permute-start(bf16[48,512]{1,0:T(8,128)(2,1)S(1)} %pad_maximum_fusion.1), channel_id=1, source_target_pairs={{0,4},{1,5},{2,6},{3,7},{4,0},{5,1},{6,2},{7,3},{8,12},{9,13},{10,... | collective-permute-start | bytes 147464 | tf_op jit(solution)/shard_map/ppermute | solution.py:283
  18.9 4.1 %collective-permute-start.1 = (bf16[48,512]{1,0:T(8,128)(2,1)S(1)}, bf16[48,512]{1,0:T(8,128)(2,1)S(1)}, u32[]{:S(2)}, u32[]{:S(2)}) collective-permute-start(bf16[48,512]{1,0:T(8,128)(2,1)S(1)} %pad_maximum_fusion.1), channel_id=1, source_target_pairs={{0,2},{1,3},{2,0},{3,1},{4,6},{5,7},{6,4},{7,5},{8,10},{9,11},{10,... | collective-permute-start | bytes 147464 | tf_op jit(solution)/shard_map/ppermute | solution.py:283
  23.0 1.5 %collective-permute-start.4 = (bf16[192,512]{1,0:T(8,128)(2,1)S(1)}, bf16[192,512]{1,0:T(8,128)(2,1)S(1)}, u32[]{:S(2)}, u32[]{:S(2)}) collective-permute-start(bf16[192,512]{1,0:T(8,128)(2,1)S(1)} %pad_maximum_fusion), channel_id=1, source_target_pairs={{0,1},{1,0},{2,3},{3,2},{4,5},{5,4},{6,7},{7,6},{8,9},{9,8},{10,11... | collective-permute-start | bytes 589832 | tf_op jit(solution)/shard_map/ppermute | solution.py:283
